TPU v7x, 128 devices: a whole 4x4x4 slice. The times are simulated.
128 devices in a mesh: tm: 4 (over z_hi, core), pair: 32 (over z_lo, y, x).
Axes of the slice: x: 4, y: 4, z: 4 (z_hi: 2, z_lo: 2; z = z_hi * 2 + z_lo), core: 2. Of those that a mesh axis runs over, the one named last changes fastest.
Arguments:
- orbitals: bfloat16 [32768, 512], P('pair', 'tm'), may hold values from -1.5 to 1.5
- level_gap: float32 [512], replicated, may hold values from 0.05 to 1.5
- screened: bfloat16 [8, 128, 1024, 1024], P('tm', 'pair'), may hold values from -0.008972168 to 0.008972168
- pair_blocks: int32 [128, 2], P('pair'), may hold values from 0 to 31, as said below
Outputs:
- self_energy: float32 [8, 512, 512], P('tm', 'pair')
Inputs may be any that keep to these rules, and one draw needn't show every extreme that they name: `pair_blocks`: each row names two point blocks a <= c; no unordered pair appears in two rows; the pair (0, 31) appears in every draw.
All inputs are finite; a program needn't handle non-finite values.
Results may differ from a plain program's by a relative error of at most 0.0049.
Values may be sent and summed in bfloat16 or wider, within the bound.
No kernel may reach another device: no remote copies, remote signals or barrier semaphores. Data moves between devices by JAX's collectives and lax.ppermute only.
A program may use at most 128 MiB of HBM per device.

v0:
```python
import jax
import jax.numpy as jnp
from jax import lax
from jax.sharding import Mesh
from jax.sharding import PartitionSpec as P

NOCC = 128
PAIR = ("pair_0", "pair_1", "pair_2")


def laid_out(tiles, dim):
    tiles = jnp.moveaxis(tiles, 0, dim)
    shape = tiles.shape
    return tiles.reshape(*shape[:dim], shape[dim] * shape[dim + 1], *shape[dim + 2 :])


def stacked_from(array, axes, sequence):
    tiles = array[None]
    for k in sequence:
        tiles = lax.all_gather(tiles, axes[k], axis=0, tiled=True)
    carried = [lax.axis_size(axes[k]) for k in reversed(sequence)]
    tiles = tiles.reshape(*carried, *array.shape)
    turned = sorted(range(len(sequence)), key=lambda place: sequence[len(sequence) - 1 - place])
    return tiles.transpose(*turned, *range(len(sequence), tiles.ndim)).reshape(-1, *array.shape)


def whole_of(array, axes, sequence, dim):
    return laid_out(stacked_from(array, axes, sequence), dim)


def split_up(array, dim, count):
    shape = array.shape
    tiles = array.reshape(*shape[:dim], count, shape[dim] // count, *shape[dim + 1 :])
    return jnp.moveaxis(tiles, dim, 0)


def sum_at_owner(array, axis, dim):
    count = lax.axis_size(axis)
    tiles = lax.all_to_all(split_up(array, dim, count), axis, 0, 0, tiled=True)
    return jnp.sum(tiles, axis=0)


def shards(orbitals, level_gap, screened, pair_blocks):
    block_rows = orbitals.shape[0]
    wanted = pair_blocks.reshape(-1)
    narrow = whole_of(orbitals, PAIR, (0, 1, 2), 0)
    picked = jnp.take(narrow.reshape(-1, block_rows, narrow.shape[1]), wanted, axis=0)
    chosen = lax.all_gather(picked, "tm", axis=2, tiled=True)
    orbital_count = chosen.shape[2]
    time_local = screened.shape[0]
    pair_local = screened.shape[1]
    time_total = time_local * lax.axis_size("tm")
    first_time = lax.axis_index("tm") * time_local
    moments = (first_time + jnp.arange(time_local)).astype(jnp.float32)
    tau = 6.0 * (moments + 0.5) / time_total
    signs = jnp.where(jnp.arange(orbital_count) < NOCC, 1.0, -1.0).astype(jnp.float32)
    factors = signs[None, :] * jnp.exp(-level_gap[None, :] * tau[:, None])
    totals = []
    for time_step in range(time_local):
        total = jnp.zeros((orbital_count, orbital_count), jnp.float32)
        for pair_step in range(pair_local):
            left = chosen[2 * pair_step]
            right = chosen[2 * pair_step + 1]
            scaled = (left.astype(jnp.float32) * factors[time_step][None, :]).astype(jnp.bfloat16)
            green = lax.dot_general(
                scaled, right, (((1,), (1,)), ((), ())), preferred_element_type=jnp.float32
            )
            product = (green * screened[time_step, pair_step].astype(jnp.float32)).astype(
                jnp.bfloat16
            )
            half = lax.dot_general(
                left, product, (((0,), (0,)), ((), ())), preferred_element_type=jnp.float32
            ).astype(jnp.bfloat16)
            block = jnp.dot(half, right, preferred_element_type=jnp.float32)
            weight = jnp.where(
                pair_blocks[pair_step, 0] == pair_blocks[pair_step, 1], 0.5, 1.0
            ).astype(jnp.float32)
            total = total + weight * (block + block.T)
        totals.append(total)
    partial_sum = jnp.stack(totals, axis=0)
    return sum_at_owner(partial_sum, PAIR, 1)


def solution(mesh):
    finer = Mesh(
        mesh.devices.reshape(mesh.shape["tm"], 2, 4, 4), ("tm", "pair_0", "pair_1", "pair_2")
    )
    placed = (P(PAIR, "tm"), P(), P("tm", PAIR, None, None), P(PAIR, None))
    return jax.shard_map(
        shards, mesh=finer, in_specs=placed, out_specs=P("tm", PAIR, None), check_vma=False
    )
```

profile of v0, /device:TPU:0, one launch (start us, length us, event | category | flops | bytes accessed | tf_op | source)
XLA Modules:
  0.0 349.6 jit_solution(2108790576608835699)
XLA Ops:
  6.5 10.9 %all-gather = bf16[2048,128]{1,0:T(8,128)(2,1)} all-gather(bf16[1024,128]{1,0:T(8,128)(2,1)} %param.4), channel_id=2, replica_groups=mesh['tm'=4,'pair_0'=2,'pair_1'=4,'pair_2'=4] {'pair_0'}, dimensions={0}, use_global_device_ids=true | all-gather | bytes 786432 | tf_op jit(solution)/shard_map/all_gather | solution.py:20
  17.6 32.8 %all-gather.5.cloned.1.call-done = bf16[8,1024,128]{2,1,0:T(8,128)(2,1)} async-done(((bf16[2,1024,128]{2,1,0:T(8,128)(2,1)}), bf16[8,1024,128]{2,1,0:T(8,128)(2,1)}) %all-gather.5.cloned.1.call-update) | async-done | bytes 2097168 | tf_op jit(solution)/shard_map/all_gather | solution.py:20
  51.4 83.7 %all-gather.7.cloned.1.call-done = bf16[32,1024,128]{2,1,0:T(8,128)(2,1)} async-done(((bf16[8,1024,128]{2,1,0:T(8,128)(2,1)}), bf16[32,1024,128]{2,1,0:T(8,128)(2,1)}) %all-gather.7.cloned.1.call-update) | async-done | bytes 8388624 | tf_op jit(solution)/shard_map/all_gather | solution.py:20
  135.1 7.5 %copy.37 = bf16[2,4,4,1024,128]{4,3,2,1,0:T(8,128)(2,1)} copy(bf16[2,4,4,1024,128]{4,3,0,1,2:T(8,128)(2,1)} %bitcast.218) | data formatting | bytes 16777216 | tf_op jit(solution)/shard_map/transpose | solution.py:24
  142.6 4.3 %gather_fusion = bf16[8,1024,128]{2,1,0:T(8,128)(2,1)S(1)} fusion(bf16[32,1024,128]{2,1,0:T(8,128)(2,1)} %bitcast.217, s32[1024]{0:T(1024)S(1)} %pad_clamp_fusion), kind=kCustom, calls=%fused_computation | custom fusion | bytes 4194336 | tf_op jit(solution)/shard_map/jit(_take)/gather | solution.py:47
  147.0 1.7 broadcast_select_fusion
  154.5 58.9 %all-gather.9.cloned.1.call-done = bf16[8,1024,512]{2,1,0:T(8,128)(2,1)} async-done(((bf16[8,1024,128]{2,1,0:T(8,128)(2,1)}), bf16[8,1024,512]{2,1,0:T(8,128)(2,1)}) %all-gather.9.cloned.1.call-update) | async-done | bytes 8388624 | tf_op jit(solution)/shard_map/all_gather | solution.py:48
  213.4 4.9 %convolution_convert_fusion.3 = bf16[512,1024]{1,0:T(8,128)(2,1)S(1)} fusion(bf16[2,4,1024,1024]{3,2,1,0:T(8,128)(2,1)} %param.6, f32[512]{0:T(512)S(1)} %bitcast.226, bf16[8,1024,512]{2,1,0:T(8,128)(2,1)} %all-gather.9.cloned.1.call-done), kind=kOutput, calls=%fused_computation.38 | convolution fusion | flops 2152726528 | bytes 6293504 | tf_op jit(solution)/shard_map/dot_general | solution.py:71
  218.3 1.9 fusion.102
  220.6 6.0 %convolution_convert_fusion.2 = bf16[512,1024]{1,0:T(8,128)(2,1)} fusion(bf16[2,4,1024,1024]{3,2,1,0:T(8,128)(2,1)} %param.6, f32[512]{0:T(512)S(1)} %bitcast.227, bf16[8,1024,512]{2,1,0:T(8,128)(2,1)} %all-gather.9.cloned.1.call-done), kind=kOutput, calls=%fused_computation.37 | convolution fusion | flops 2152726528 | bytes 6293504 | tf_op jit(solution)/shard_map/dot_general | solution.py:71
  226.5 2.2 fusion.104
  228.8 1.4 copy.44
  230.2 5.9 %convolution_convert_fusion = bf16[512,1024]{1,0:T(8,128)(2,1)} fusion(bf16[2,4,1024,1024]{3,2,1,0:T(8,128)(2,1)} %param.6, f32[512]{0:T(512)S(1)} %bitcast.228, bf16[8,1024,512]{2,1,0:T(8,128)(2,1)} %all-gather.9.cloned.1.call-done), kind=kOutput, calls=%fused_computation.35 | convolution fusion | flops 2152726528 | bytes 6293504 | tf_op jit(solution)/shard_map/dot_general | solution.py:71
  236.1 3.2 fusion.108
  239.3 2.5 copy.46
  241.8 6.0 %convolution_convert_fusion.1 = bf16[512,1024]{1,0:T(8,128)(2,1)} fusion(bf16[2,4,1024,1024]{3,2,1,0:T(8,128)(2,1)} %param.6, f32[512]{0:T(512)S(1)} %bitcast.229, bf16[8,1024,512]{2,1,0:T(8,128)(2,1)} %all-gather.9.cloned.1.call-done), kind=kOutput, calls=%fused_computation.36 | convolution fusion | flops 2152726528 | bytes 6293504 | tf_op jit(solution)/shard_map/dot_general | solution.py:71
  247.8 3.2 fusion.106
  251.0 2.8 copy.45
  253.8 5.9 %convolution_convert_fusion.4 = bf16[512,1024]{1,0:T(8,128)(2,1)} fusion(bf16[2,4,1024,1024]{3,2,1,0:T(8,128)(2,1)} %param.6, f32[512]{0:T(512)S(1)} %bitcast.222, bf16[8,1024,512]{2,1,0:T(8,128)(2,1)} %all-gather.9.cloned.1.call-done), kind=kOutput, calls=%fused_computation.39 | convolution fusion | flops 2152726528 | bytes 6293504 | tf_op jit(solution)/shard_map/dot_general | solution.py:71
  259.7 3.2 fusion.109
  262.9 2.5 copy.42
  265.5 5.9 %convolution_convert_fusion.5 = bf16[512,1024]{1,0:T(8,128)(2,1)} fusion(bf16[2,4,1024,1024]{3,2,1,0:T(8,128)(2,1)} %param.6, f32[512]{0:T(512)S(1)} %bitcast.223, bf16[8,1024,512]{2,1,0:T(8,128)(2,1)} %all-gather.9.cloned.1.call-done), kind=kOutput, calls=%fused_computation.40 | convolution fusion | flops 2152726528 | bytes 6293504 | tf_op jit(solution)/shard_map/dot_general | solution.py:71
  271.4 3.2 fusion.107
  274.6 2.5 copy.41
  277.2 5.9 %convolution_convert_fusion.7 = bf16[512,1024]{1,0:T(8,128)(2,1)} fusion(bf16[2,4,1024,1024]{3,2,1,0:T(8,128)(2,1)} %param.6, f32[512]{0:T(512)S(1)} %bitcast.224, bf16[8,1024,512]{2,1,0:T(8,128)(2,1)} %all-gather.9.cloned.1.call-done), kind=kOutput, calls=%fused_computation.42 | convolution fusion | flops 2152726528 | bytes 6293504 | tf_op jit(solution)/shard_map/dot_general | solution.py:71
  283.1 3.2 fusion.103
  286.3 2.5 copy.39
  288.8 5.9 %convolution_convert_fusion.6 = bf16[512,1024]{1,0:T(8,128)(2,1)} fusion(bf16[2,4,1024,1024]{3,2,1,0:T(8,128)(2,1)} %param.6, f32[512]{0:T(512)S(1)} %bitcast.225, bf16[8,1024,512]{2,1,0:T(8,128)(2,1)} %all-gather.9.cloned.1.call-done), kind=kOutput, calls=%fused_computation.41 | convolution fusion | flops 2152726528 | bytes 6293504 | tf_op jit(solution)/shard_map/dot_general | solution.py:71
  294.7 3.3 fusion.105
  298.0 2.5 copy.40
  300.6 3.7 %fusion.33 = f32[512,512]{1,0:T(8,128)S(1)} fusion(f32[512,512]{1,0:T(8,128)} %fusion.108, f32[512,512]{0,1:T(8,128)} %copy.46, f32[512,512]{1,0:T(8,128)} %fusion.106, f32[512,512]{0,1:T(8,128)} %copy.45, f32[512,512]{1,0:T(8,128)S(1)} %fusion.104, f32[512,512]{0,1:T(8,128)} %copy.44, f32[512,512]{1,0:T(8,128)S(1)} %fusion.102, f32[512,512]{0,1:T(8,128)S(1)} %copy.43, ...), kind=kLoop, calls=%fused_computation.57 | loop fusion | flops 2883584 | bytes 9437200 | tf_op jit(solution)/shard_map/add | solution.py:78
  306.8 35.5 %all_to_all.5 = f32[32,2,16,512]{3,2,1,0:T(8,128)S(1)} all-to-all(f32[32,2,16,512]{3,2,1,0:T(8,128)S(1)} %maximum_bitcast_fusion), channel_id=1, replica_groups=mesh['tm'=4,'pair_0'=2,'pair_1'=4,'pair_2'=4] {'pair_0','pair_1','pair_2'}, dimensions={0} | all-to-all | bytes 4194304 | tf_op jit(solution)/shard_map/all_to_all | solution.py:39
  (42 shorter events, 5.4 us)
Async XLA Ops:
  6.5 43.8 %all-gather.5.cloned.1.call-start = ((), (), s32[]{:S(2)}) async-start(), calls=%async_computation.1 | async-start | bytes 2621440 | tf_op jit(solution)/shard_map/all_gather | solution.py:20
  17.5 117.6 %all-gather.7.cloned.1.call-start = ((), (), s32[]{:S(2)}) async-start(), calls=%async_computation.2 | async-start | bytes 10485760 | tf_op jit(solution)/shard_map/all_gather | solution.py:20
  50.4 163.0 %all-gather.9.cloned.1.call-start = ((), (), s32[]{:S(2)}) async-start(), calls=%async_computation.3 | async-start | bytes 10485760 | tf_op jit(solution)/shard_map/all_gather | solution.py:48
  147.0 1.7 copy-start.9
  147.0 1.7 copy-start.8
  300.5 3.8 %copy-start = (f32[512,512]{1,0:T(8,128)S(1)}, f32[512,512]{1,0:T(8,128)}, u32[]{:S(2)}) copy-start(f32[512,512]{1,0:T(8,128)} %fusion.109) | copy-start | bytes 3145732
  300.5 3.8 %copy-start.1 = (f32[512,512]{0,1:T(8,128)S(1)}, f32[512,512]{0,1:T(8,128)}, u32[]{:S(2)}) copy-start(f32[512,512]{0,1:T(8,128)} %copy.42) | copy-start | bytes 3145732
  300.5 3.8 %copy-start.2 = (f32[512,512]{1,0:T(8,128)S(1)}, f32[512,512]{1,0:T(8,128)}, u32[]{:S(2)}) copy-start(f32[512,512]{1,0:T(8,128)} %fusion.107) | copy-start | bytes 3145732
  300.5 3.8 %copy-start.3 = (f32[512,512]{0,1:T(8,128)S(1)}, f32[512,512]{0,1:T(8,128)}, u32[]{:S(2)}) copy-start(f32[512,512]{0,1:T(8,128)} %copy.41) | copy-start | bytes 3145732
  300.5 4.1 %copy-start.4 = (f32[512,512]{1,0:T(8,128)S(1)}, f32[512,512]{1,0:T(8,128)}, u32[]{:S(2)}) copy-start(f32[512,512]{1,0:T(8,128)} %fusion.103) | copy-start | bytes 3145732
  300.6 4.4 %copy-start.5 = (f32[512,512]{0,1:T(8,128)S(1)}, f32[512,512]{0,1:T(8,128)}, u32[]{:S(2)}) copy-start(f32[512,512]{0,1:T(8,128)} %copy.39) | copy-start | bytes 3145732
  300.6 4.7 %copy-start.6 = (f32[512,512]{1,0:T(8,128)S(1)}, f32[512,512]{1,0:T(8,128)}, u32[]{:S(2)}) copy-start(f32[512,512]{1,0:T(8,128)} %fusion.105) | copy-start | bytes 3145732
  300.6 4.9 %copy-start.7 = (f32[512,512]{0,1:T(8,128)S(1)}, f32[512,512]{0,1:T(8,128)}, u32[]{:S(2)}) copy-start(f32[512,512]{0,1:T(8,128)} %copy.40) | copy-start | bytes 3145732
Sparse Core Ops, SparseCore 0:
  17.6 32.7 all-gather.4
  52.0 83.0 all-gather.6
  148.8 64.5 all-gather.8
where the time goes:
time: 350 us
  waiting for transfers between devices  175 us (50%)
  matrix products  70 us (20%)
  blocking collectives  46.5 us (13%)
  local copies, waits for them, and re-layouts  31.8 us (9%)
  between operations  18.3 us (5%)
  other arithmetic  7.55 us (2%)
    all_gather x2, waiting for transfers between devices, stacked_from(): tiles = lax.all_gather(tiles, axes[k], axis=0, tiled=True)  117 us
    all_gather x1, waiting for transfers between devices, shards(): chosen = lax.all_gather(picked, 'tm', axis=2, tiled=True)  58.9 us
    dot_general x8, matrix products, shards(): lax.dot_general(left, product, (((0,), (0,)), ((), ())), preferred_elemen...  46.3 us
    all_to_all x1, blocking collectives, sum_at_owner(): tiles = lax.all_to_all(split_up(array, dim, count), axis, 0, 0, tiled=True)  35.5 us
    dot_general x8, matrix products, shards(): block = jnp.dot(half, right, preferred_element_type=jnp.float32)  23.6 us
    dot_general x8, local copies, waits for them, and re-layouts, shards(): block = jnp.dot(half, right, preferred_element_type=jnp.float32)  17.2 us
    all_gather x1, blocking collectives, stacked_from(): tiles = lax.all_gather(tiles, axes[k], axis=0, tiled=True)  10.9 us
    transpose x1, local copies, waits for them, and re-layouts, stacked_from(): tiles.transpose(*turned, *range(len(sequence), tiles.ndim))  7.53 us
  transfers between devices with their start and end apart: 3, of which 3 were waited for; matrix products, arithmetic and copies ran while one was open for 0% of the time, Pallas kernels for 0%

commit v1 on v0

v1 whole, which is shorter than its diff:
```python
import jax
import jax.numpy as jnp
from jax import lax
from jax.experimental import pallas as pl
from jax.experimental.pallas import tpu as pltpu
from jax.sharding import Mesh
from jax.sharding import PartitionSpec as P

NOCC = 128
PAIR = ("zl", "y", "x")
SAME_CORE = ("zh", "zl", "y", "x")
CHUNKS = ((0, 2), (2, 2))
INDEX_ROWS = 8


def picked_for(wants, slices, first, count):
    owners, rows, cols = slices.shape[0], slices.shape[1] - INDEX_ROWS, slices.shape[2]
    per_step = 8

    def kernel(wants_ref, slices_ref, out_ref):
        step = pl.program_id(1)
        for d in range(per_step):
            for k in range(count):
                block = wants_ref[step * per_step + d, first + k]
                out_ref[0, d, k] = slices_ref[block, :rows, :]

    return pl.pallas_call(
        kernel,
        grid_spec=pltpu.PrefetchScalarGridSpec(
            num_scalar_prefetch=1,
            grid=(2, owners // per_step),
            in_specs=[pl.BlockSpec(slices.shape, lambda h, i, w: (0, 0, 0))],
            out_specs=pl.BlockSpec((1, per_step, count, rows, cols), lambda h, i, w: (h, i, 0, 0, 0)),
        ),
        out_shape=jax.ShapeDtypeStruct((2, owners, count, rows, cols), slices.dtype),
        compiler_params=pltpu.CompilerParams(dimension_semantics=("arbitrary", "arbitrary")),
    )(wants, slices)


def pair_sums(core, factors, mine, other, screened, first, pairs, carried, last):
    _, slots, _, rows, cols = mine.shape
    times, _, blk, _ = screened.shape
    norb = factors.shape[-1]
    strip = 256

    def kernel(core_ref, *refs):
        if carried is None:
            fac, mine_ref, other_ref, tile, out, left, right, left_t, inner, acc = refs
        else:
            fac, mine_ref, other_ref, tile, start, out, left, right, left_t, inner, acc = refs
        p = pl.program_id(0)
        t = pl.program_id(1)
        own = core_ref[0]

        @pl.when((p == 0) & (t == 0))
        def _():
            if carried is None:
                acc[...] = jnp.zeros(acc.shape, acc.dtype)
            else:
                acc[...] = start[...]

        @pl.when(t == 0)
        def _():
            for source, side in ((mine_ref, own), (other_ref, 1 - own)):
                for half in range(2):
                    at = pl.multiple_of((half * 2 + side) * cols, cols)
                    left[:, pl.ds(at, cols)] = source[half, :, 0].reshape(blk, cols)
                    right[:, pl.ds(at, cols)] = source[half, :, 1].reshape(blk, cols)
            left_t[...] = left[...].T

        scale = fac[0, pl.ds(t, 1), :]
        whole = right[...]
        for s in range(blk // strip):
            part = slice(s * strip, (s + 1) * strip)
            scaled = (left[part, :].astype(jnp.float32) * scale).astype(jnp.bfloat16)
            green = lax.dot_general(
                scaled, whole, (((1,), (1,)), ((), ())), preferred_element_type=jnp.float32
            )
            product = (green * tile[0, 0, part, :].astype(jnp.float32)).astype(jnp.bfloat16)
            inner[part, :] = jnp.dot(product, whole, preferred_element_type=jnp.float32).astype(
                jnp.bfloat16
            )
        acc[t] += jnp.dot(left_t[...], inner[...], preferred_element_type=jnp.float32)

        @pl.when(p == pairs - 1)
        def _():
            total = acc[t]
            if last:
                both = (total + total.T).astype(out.dtype)
                out[:, t] = both.reshape(out.shape[0], out.shape[2], norb)
            else:
                out[t] = total

    own_rows = norb // slots
    if last:
        out_shape = jax.ShapeDtypeStruct((slots, times, own_rows, norb), jnp.bfloat16)
    else:
        out_shape = jax.ShapeDtypeStruct((times, norb, norb), jnp.float32)
    ends = len(out_shape.shape)
    blocks = pl.BlockSpec((2, slots, 2, rows, cols), lambda p, t, c: (0, 0, p, 0, 0))
    in_specs = [
        pl.BlockSpec((1, times, norb), lambda p, t, c: (first + p, 0, 0)),
        blocks,
        blocks,
        pl.BlockSpec((1, 1, blk, blk), lambda p, t, c: (t, first + p, 0, 0)),
    ]
    operands = [core, factors, mine, other, screened]
    if carried is not None:
        in_specs.append(pl.BlockSpec(carried.shape, lambda p, t, c: (0, 0, 0)))
        operands.append(carried)
    return pl.pallas_call(
        kernel,
        grid_spec=pltpu.PrefetchScalarGridSpec(
            num_scalar_prefetch=1,
            grid=(pairs, times),
            in_specs=in_specs,
            out_specs=pl.BlockSpec(out_shape.shape, lambda p, t, c: (0,) * ends),
            scratch_shapes=[
                pltpu.VMEM((blk, norb), jnp.bfloat16),
                pltpu.VMEM((blk, norb), jnp.bfloat16),
                pltpu.VMEM((norb, blk), jnp.bfloat16),
                pltpu.VMEM((blk, norb), jnp.bfloat16),
                pltpu.VMEM((times, norb, norb), jnp.float32),
            ],
        ),
        out_shape=out_shape,
        compiler_params=pltpu.CompilerParams(
            vmem_limit_bytes=48 << 20, dimension_semantics=("arbitrary", "arbitrary")
        ),
    )(*operands)


def shards(orbitals, level_gap, screened, pair_blocks):
    owners = lax.axis_size(PAIR)
    cols = orbitals.shape[1]
    rows = orbitals.shape[0] // owners
    time_local, pair_local = screened.shape[:2]
    norb = level_gap.shape[0]

    asked = jnp.zeros((INDEX_ROWS, cols), jnp.bfloat16)
    asked = asked.at[0, : 2 * pair_local].set(pair_blocks.reshape(-1).astype(jnp.bfloat16))
    sent = jnp.concatenate(
        [
            orbitals.reshape(owners, rows, cols),
            jnp.broadcast_to(asked, (owners, INDEX_ROWS, cols)),
        ],
        axis=1,
    )
    slices = lax.all_to_all(sent, PAIR, 0, 0, tiled=True)
    wants = slices[:, rows, : 2 * pair_local].astype(jnp.int32)

    group = lax.axis_index(("zh", "core"))
    core = lax.axis_index("core").astype(jnp.int32).reshape(1)
    moments = (group * time_local + jnp.arange(time_local)).astype(jnp.float32)
    tau = 6.0 * (moments + 0.5) / (time_local * lax.axis_size(("zh", "core")))
    signs = jnp.where(jnp.arange(norb) < NOCC, 1.0, -1.0).astype(jnp.float32)
    weights = jnp.where(pair_blocks[:, 0] == pair_blocks[:, 1], 0.5, 1.0).astype(jnp.float32)
    factors = signs[None, :] * jnp.exp(-level_gap[None, :] * tau[:, None])
    factors = weights[:, None, None] * factors[None]

    total = None
    for first, pairs in CHUNKS:
        picked = picked_for(wants, slices, 2 * first, 2 * pairs)
        picked = picked.reshape(2 * owners, 2 * pairs, rows, cols)
        mine = lax.all_to_all(picked, SAME_CORE, 0, 0, tiled=True)
        other = lax.ppermute(mine, "core", [(0, 1), (1, 0)])
        shape = (2, owners, 2 * pairs, rows, cols)
        last = first + pairs == pair_local
        total = pair_sums(
            core, factors, mine.reshape(shape), other.reshape(shape), screened, first, pairs, total, last
        )
    shares = lax.all_to_all(total, PAIR, 0, 0, tiled=True)
    return jnp.sum(shares.astype(jnp.float32), axis=0)


def solution(mesh):
    fine = Mesh(mesh.devices.reshape(2, 2, 2, 4, 4), ("zh", "core", "zl", "y", "x"))
    tm = ("zh", "core")
    placed = (P(PAIR, tm), P(), P(tm, PAIR, None, None), P(PAIR, None))
    return jax.shard_map(
        shards, mesh=fine, in_specs=placed, out_specs=P(tm, PAIR, None), check_vma=False
    )
```

time: 350 us -> 152 us (0.43)
  waiting for transfers between devices: 175 us -> 50.8 us
  matrix products: 70 us -> 0 us
  Pallas kernels: 0 us -> 42.7 us
  local copies, waits for them, and re-layouts: 31.8 us -> 1.61 us
  between operations: 18.3 us -> 0.1 us
  starting transfers between devices: 0.08 us -> 13.8 us
  blocking collectives: 46.5 us -> 39.4 us
  other arithmetic: 7.55 us -> 3.29 us
    all_gather x3 -> x0, waiting for transfers between devices: 175 us -> none  [the longest x2 117 us: stacked_from(): tiles = lax.all_gather(tiles, axes[k], axis=0, tiled=True)]
    dot_general x16 -> x0, matrix products: 70 us -> none  [the longest x8 46.3 us: shards(): lax.dot_general(left, product, (((0,), (0,)), ((), ())), preferred_elemen...]
    all_to_all x0 -> x2, waiting for transfers between devices: none -> 50.8 us  [shards(): mine = lax.all_to_all(picked, SAME_CORE, 0, 0, tiled=True)]
    pallas_call x0 -> x4, Pallas kernels: none -> 42.7 us  [the longest x2 32.9 us: pair_sums(): pl.pallas_call(kernel, grid_spec=pltpu.PrefetchScalarGridSpec(num_scalar_...]
    dot_general x8 -> x0, local copies, waits for them, and re-layouts: 17.2 us -> none  [shards(): block = jnp.dot(half, right, preferred_element_type=jnp.float32)]
    all_to_all x0 -> x2, starting transfers between devices: none -> 13.7 us  [shards(): mine = lax.all_to_all(picked, SAME_CORE, 0, 0, tiled=True)]
    all_gather x1 -> x0, blocking collectives: 10.9 us -> none  [stacked_from(): tiles = lax.all_gather(tiles, axes[k], axis=0, tiled=True)]
    transpose x1 -> x0, local copies, waits for them, and re-layouts: 7.53 us -> none  [stacked_from(): tiles.transpose(*turned, *range(len(sequence), tiles.ndim))]
  transfers between devices with their start and end apart: 3 -> 4, of which waited for: 3 -> 2; matrix products, arithmetic and copies ran while one was open for 0% -> 0% of each run, Pallas kernels for 0% -> 14%
where the time goes in v1:
time: 152 us
  waiting for transfers between devices  50.8 us (33%)
  Pallas kernels  42.7 us (28%)
  blocking collectives  39.4 us (26%)
  starting transfers between devices  13.8 us (9%)
  other arithmetic  3.29 us (2%)
  local copies, waits for them, and re-layouts  1.61 us (1%)
    all_to_all x2, waiting for transfers between devices, shards(): mine = lax.all_to_all(picked, SAME_CORE, 0, 0, tiled=True)  50.8 us
    pallas_call x2, Pallas kernels, pair_sums(): pl.pallas_call(kernel, grid_spec=pltpu.PrefetchScalarGridSpec(num_scalar_...  32.9 us
    all_to_all x1, blocking collectives, shards(): shares = lax.all_to_all(total, PAIR, 0, 0, tiled=True)  21.4 us
    all_to_all x1, blocking collectives, shards(): slices = lax.all_to_all(sent, PAIR, 0, 0, tiled=True)  18 us
    all_to_all x2, starting transfers between devices, shards(): mine = lax.all_to_all(picked, SAME_CORE, 0, 0, tiled=True)  13.7 us
    pallas_call x2, Pallas kernels, picked_for(): pl.pallas_call(kernel, grid_spec=pltpu.PrefetchScalarGridSpec(num_scalar_...  9.85 us
  transfers between devices with their start and end apart: 4, of which 2 were waited for; matrix products, arithmetic and copies ran while one was open for 0% of the time, Pallas kernels for 14%

profile of v1, /device:TPU:0, one launch (start us, length us, event | category | flops | bytes accessed | tf_op | source)
XLA Modules:
  0.0 151.8 jit_solution(2206731243822226773)
XLA Ops:
  0.0 0.7 convert_element_type.27
  0.7 0.1 copy.6
  0.8 0.1 convert_element_type.28
  0.9 1.0 pad_maximum_fusion
  1.9 18.0 %all_to_all.20.slices_ref = bf16[32,40,128]{2,1,0:T(8,128)(2,1)S(1)} all-to-all(bf16[32,40,128]{2,1,0:T(8,128)(2,1)S(1)} %pad_maximum_fusion), channel_id=1, replica_groups=mesh['zh'=2,'core'=2,'zl'=2,'y'=4,'x'=4] {'zl','y','x'}, dimensions={0} | all-to-all | bytes 655360 | tf_op jit(solution)/shard_map/all_to_all | solution.py:149
  19.9 0.0 copy-start.1
  19.9 0.7 slice_convert_fusion
  20.6 0.1 copy-done.1
  20.7 4.9 %shard_map.47 = bf16[2,32,4,32,128]{4,3,2,1,0:T(8,128)(2,1)} custom-call(s32[32,8]{1,0:T(8,128)} %bitcast.15, bf16[32,40,128]{2,1,0:T(8,128)(2,1)} %copy-done.1), custom_call_target="tpu_custom_call" | custom-call | tf_op jit(solution)/shard_map/pallas_call | solution.py:27
  25.6 7.9 %all-to-all-start.2 = ((bf16[64,4,32,128]{3,2,1,0:T(8,128)(2,1)}), bf16[64,4,32,128]{3,2,1,0:T(8,128)(2,1)S(1)}, u32[]{:S(2)}, u32[]{:S(2)}) async-start(bf16[64,4,32,128]{3,2,1,0:T(8,128)(2,1)} %bitcast.13), calls=%async_computation.2 | async-start | bytes 4194304 | tf_op jit(solution)/shard_map/all_to_all | solution.py:165
  33.5 4.9 %shard_map.46 = bf16[2,32,4,32,128]{4,3,2,1,0:T(8,128)(2,1)} custom-call(s32[32,8]{1,0:T(8,128)} %bitcast.16, bf16[32,40,128]{2,1,0:T(8,128)(2,1)} %copy-done.1), custom_call_target="tpu_custom_call" | custom-call | tf_op jit(solution)/shard_map/pallas_call | solution.py:27
  38.4 23.6 %all-to-all-done.2 = bf16[64,4,32,128]{3,2,1,0:T(8,128)(2,1)S(1)} async-done(((bf16[64,4,32,128]{3,2,1,0:T(8,128)(2,1)}), bf16[64,4,32,128]{3,2,1,0:T(8,128)(2,1)S(1)}, u32[]{:S(2)}, u32[]{:S(2)}) %all-to-all-start.2) | async-done | bytes 2097184 | tf_op jit(solution)/shard_map/all_to_all | solution.py:165
  62.0 0.0 copy-start.2
  62.0 0.0 copy-start.3
  62.0 5.9 %all-to-all-start.1 = ((bf16[64,4,32,128]{3,2,1,0:T(8,128)(2,1)}), bf16[64,4,32,128]{3,2,1,0:T(8,128)(2,1)}, u32[]{:S(2)}, u32[]{:S(2)}) async-start(bf16[64,4,32,128]{3,2,1,0:T(8,128)(2,1)} %bitcast.12), calls=%async_computation.1 | async-start | bytes 4194304 | tf_op jit(solution)/shard_map/all_to_all | solution.py:165
  67.9 0.1 collective-permute-start.1
  68.0 27.2 %all-to-all-done.1 = bf16[64,4,32,128]{3,2,1,0:T(8,128)(2,1)} async-done(((bf16[64,4,32,128]{3,2,1,0:T(8,128)(2,1)}), bf16[64,4,32,128]{3,2,1,0:T(8,128)(2,1)}, u32[]{:S(2)}, u32[]{:S(2)}) %all-to-all-start.1) | async-done | bytes 2097184 | tf_op jit(solution)/shard_map/all_to_all | solution.py:165
  95.2 0.0 collective-permute-start
  95.2 0.0 copy-done.2
  95.2 0.0 copy-done.3
  95.3 0.1 exponential_multiply_fusion
  95.3 0.1 broadcast_multiply_fusion.refs_0_
  95.4 0.0 collective-permute-done.1
  95.4 15.8 %shard_map.48.refs_4_ = f32[2,512,512]{2,1,0:T(8,128)S(1)} custom-call(s32[1]{0:T(128)} %bitcast.core_ref, f32[4,2,512]{2,1,0:T(2,128)S(1)} %broadcast_multiply_fusion.refs_0_, bf16[2,32,4,32,128]{4,3,2,1,0:T(8,128)(2,1)S(1)} %bitcast.11, bf16[2,32,4,32,128]{4,3,2,1,0:T(8,128)(2,1)} %bitcast.9.refs_2_, bf16[2,4,1024,1024]{3,2,1,0:T(8,128)(2,1)} %refs_3_.3), custom_call_target="tpu_custom_call" | custom-call | tf_op jit(solution)/shard_map/pallas_call | solution.py:111
  111.2 0.0 copy-start
  111.2 1.3 copy-done
  112.5 0.0 collective-permute-done
  112.5 17.1 %shard_map.49 = bf16[32,2,16,512]{3,2,1,0:T(8,128)(2,1)S(1)} custom-call(s32[1]{0:T(128)} %bitcast.core_ref, f32[4,2,512]{2,1,0:T(2,128)S(1)} %broadcast_multiply_fusion.refs_0_, bf16[2,32,4,32,128]{4,3,2,1,0:T(8,128)(2,1)} %bitcast.5.refs_1_, bf16[2,32,4,32,128]{4,3,2,1,0:T(8,128)(2,1)} %bitcast.6.refs_2_, bf16[2,4,1024,1024]{3,2,1,0:T(8,128)(2,1)} %refs_3_.3, ...), custom_call_target="tpu_custom_call" | custom-call | tf_op jit(solution)/shard_map/pallas_call | solution.py:111
  129.6 21.4 %all_to_all.21 = bf16[32,2,16,512]{3,2,1,0:T(8,128)(2,1)S(1)} all-to-all(bf16[32,2,16,512]{3,2,1,0:T(8,128)(2,1)S(1)} %shard_map.49), channel_id=1, replica_groups=mesh['zh'=2,'core'=2,'zl'=2,'y'=4,'x'=4] {'zl','y','x'}, dimensions={0} | all-to-all | bytes 2097152 | tf_op jit(solution)/shard_map/all_to_all | solution.py:172
  151.0 0.8 convert_reduce_fusion
  (6 shorter events, 0.0 us)
Async XLA Ops:
  19.9 0.7 copy-start.1
  25.6 36.4 %all-to-all-start.2 = ((bf16[64,4,32,128]{3,2,1,0:T(8,128)(2,1)}), bf16[64,4,32,128]{3,2,1,0:T(8,128)(2,1)S(1)}, u32[]{:S(2)}, u32[]{:S(2)}) async-start(bf16[64,4,32,128]{3,2,1,0:T(8,128)(2,1)} %bitcast.13), calls=%async_computation.2 | async-start | bytes 4194304 | tf_op jit(solution)/shard_map/all_to_all | solution.py:165
  62.0 33.2 %copy-start.2 = (f32[512]{0:T(512)S(1)}, f32[512]{0:T(512)}, u32[]{:S(2)}) copy-start(f32[512]{0:T(512)} %param.7) | copy-start | bytes 6148
  62.0 33.2 %copy-start.3 = (s32[4,2]{0,1:T(2,128)S(1)}, s32[4,2]{0,1:T(2,128)}, u32[]{:S(2)}) copy-start(s32[4,2]{0,1:T(2,128)} %param.9) | copy-start | bytes 100
  62.0 33.2 %all-to-all-start.1 = ((bf16[64,4,32,128]{3,2,1,0:T(8,128)(2,1)}), bf16[64,4,32,128]{3,2,1,0:T(8,128)(2,1)}, u32[]{:S(2)}, u32[]{:S(2)}) async-start(bf16[64,4,32,128]{3,2,1,0:T(8,128)(2,1)} %bitcast.12), calls=%async_computation.1 | async-start | bytes 4194304 | tf_op jit(solution)/shard_map/all_to_all | solution.py:165
  67.9 27.5 %collective-permute-start.1 = (bf16[64,4,32,128]{3,2,1,0:T(8,128)(2,1)S(1)}, bf16[64,4,32,128]{3,2,1,0:T(8,128)(2,1)}, u32[]{:S(2)}, u32[]{:S(2)}) collective-permute-start(bf16[64,4,32,128]{3,2,1,0:T(8,128)(2,1)S(1)} %all-to-all-done.2), channel_id=1, source_target_pairs={{0,32},{32,0},{1,33},{33,1},{2,34},{34,2},{3,35},{35,3},{4,36},{36... | collective-permute-start | bytes 6291464 | tf_op jit(solution)/shard_map/ppermute | solution.py:166
  95.2 17.3 %collective-permute-start = (bf16[64,4,32,128]{3,2,1,0:T(8,128)(2,1)}, bf16[64,4,32,128]{3,2,1,0:T(8,128)(2,1)}, u32[]{:S(2)}, u32[]{:S(2)}) collective-permute-start(bf16[64,4,32,128]{3,2,1,0:T(8,128)(2,1)} %all-to-all-done.1), channel_id=1, source_target_pairs={{0,32},{32,0},{1,33},{33,1},{2,34},{34,2},{3,35},{35,3},{4,36},{36... | collective-permute-start | bytes 6291464 | tf_op jit(solution)/shard_map/ppermute | solution.py:166
  111.2 1.3 copy-start

commit v2 on v1

--- a/solution.py
+++ b/solution.py
@@ -9,55 +9,69 @@
 NOCC = 128
 PAIR = ("zl", "y", "x")
 SAME_CORE = ("zh", "zl", "y", "x")
-CHUNKS = ((0, 2), (2, 2))
+CHUNKS = ((0, 3), (3, 1))
 INDEX_ROWS = 8
+
+
+def in_hbm(array):
+    return pltpu.with_memory_space_constraint(array, pltpu.HBM)
 
 
 def picked_for(wants, slices, first, count):
     owners, rows, cols = slices.shape[0], slices.shape[1] - INDEX_ROWS, slices.shape[2]
-    per_step = 8
-
-    def kernel(wants_ref, slices_ref, out_ref):
-        step = pl.program_id(1)
-        for d in range(per_step):
-            for k in range(count):
-                block = wants_ref[step * per_step + d, first + k]
-                out_ref[0, d, k] = slices_ref[block, :rows, :]
+    per_step = 4
+
+    def kernel(wants_ref, slices_ref, out_ref, sent):
+        def some(i, unused):
+            for d in range(per_step):
+                for k in range(count):
+                    block = wants_ref[i * per_step + d, first + k]
+                    piece = slices_ref.at[block, pl.ds(0, rows), :]
+                    for half in range(2):
+                        at = out_ref.at[half, i * per_step + d, k]
+                        pltpu.make_async_copy(piece, at, sent).start()
+            return unused
+
+        lax.fori_loop(0, owners // per_step, some, 0)
+        pltpu.make_async_copy(out_ref, out_ref, sent).wait()
 
     return pl.pallas_call(
         kernel,
         grid_spec=pltpu.PrefetchScalarGridSpec(
             num_scalar_prefetch=1,
-            grid=(2, owners // per_step),
-            in_specs=[pl.BlockSpec(slices.shape, lambda h, i, w: (0, 0, 0))],
-            out_specs=pl.BlockSpec((1, per_step, count, rows, cols), lambda h, i, w: (h, i, 0, 0, 0)),
+            grid=(1,),
+            in_specs=[pl.BlockSpec(memory_space=pltpu.VMEM)],
+            out_specs=pl.BlockSpec(memory_space=pltpu.HBM),
+            scratch_shapes=[pltpu.SemaphoreType.DMA(())],
         ),
-        out_shape=jax.ShapeDtypeStruct((2, owners, count, rows, cols), slices.dtype),
-        compiler_params=pltpu.CompilerParams(dimension_semantics=("arbitrary", "arbitrary")),
+        out_shape=pltpu.HBM((2, owners, count, rows, cols), slices.dtype),
+        compiler_params=pltpu.CompilerParams(vmem_limit_bytes=16 << 20),
     )(wants, slices)
 
 
-def pair_sums(core, factors, mine, other, screened, first, pairs, carried, last):
-    _, slots, _, rows, cols = mine.shape
+def pair_sums(core, factors, mine, other, screened, first, carried, last):
+    _, slots, blocks, rows, cols = mine.shape
+    pairs = blocks // 2
     times, _, blk, _ = screened.shape
     norb = factors.shape[-1]
     strip = 256
 
-    def kernel(core_ref, *refs):
-        if carried is None:
-            fac, mine_ref, other_ref, tile, out, left, right, left_t, inner, acc = refs
-        else:
-            fac, mine_ref, other_ref, tile, start, out, left, right, left_t, inner, acc = refs
+    def kernel(core_ref, fac, mine_ref, other_ref, tile, *refs):
+        start = None
+        if carried is not None:
+            start, *refs = refs
+        out, left, right, left_t, inner, acc, moved = refs
         p = pl.program_id(0)
         t = pl.program_id(1)
         own = core_ref[0]
-
-        @pl.when((p == 0) & (t == 0))
+        opens = (p == 0) & (t == 0)
+
+        @pl.when(opens)
         def _():
-            if carried is None:
+            if start is None:
                 acc[...] = jnp.zeros(acc.shape, acc.dtype)
             else:
-                acc[...] = start[...]
+                pltpu.make_async_copy(start, acc, moved.at[0]).start()
 
         @pl.when(t == 0)
         def _():
@@ -80,52 +94,71 @@
             inner[part, :] = jnp.dot(product, whole, preferred_element_type=jnp.float32).astype(
                 jnp.bfloat16
             )
+
+        if start is not None:
+
+            @pl.when(opens)
+            def _():
+                pltpu.make_async_copy(start, acc, moved.at[0]).wait()
+
         acc[t] += jnp.dot(left_t[...], inner[...], preferred_element_type=jnp.float32)
 
-        @pl.when(p == pairs - 1)
-        def _():
-            total = acc[t]
-            if last:
+        if last:
+
+            @pl.when(p == pairs - 1)
+            def _():
+                total = acc[t]
                 both = (total + total.T).astype(out.dtype)
                 out[:, t] = both.reshape(out.shape[0], out.shape[2], norb)
-            else:
-                out[t] = total
-
-    own_rows = norb // slots
+
+        else:
+
+            @pl.when(p == pairs - 1)
+            def _():
+                pltpu.make_async_copy(acc.at[t], out.at[t], moved.at[t]).start()
+
+            @pl.when((p == pairs - 1) & (t == times - 1))
+            def _():
+                for k in range(times):
+                    pltpu.make_async_copy(acc.at[k], out.at[k], moved.at[k]).wait()
+
+    sums = (times, norb, norb)
     if last:
-        out_shape = jax.ShapeDtypeStruct((slots, times, own_rows, norb), jnp.bfloat16)
+        out_shape = jax.ShapeDtypeStruct((slots, times, norb // slots, norb), jnp.bfloat16)
+        out_spec = pl.BlockSpec(out_shape.shape, lambda p, t, c: (0, 0, 0, 0))
     else:
-        out_shape = jax.ShapeDtypeStruct((times, norb, norb), jnp.float32)
-    ends = len(out_shape.shape)
-    blocks = pl.BlockSpec((2, slots, 2, rows, cols), lambda p, t, c: (0, 0, p, 0, 0))
+        out_shape = pltpu.HBM(sums, jnp.float32)
+        out_spec = pl.BlockSpec(memory_space=pltpu.HBM)
+    operands = [core, factors, mine, other, in_hbm(screened)]
+    brought = pl.BlockSpec((2, slots, 2, rows, cols), lambda p, t, c: (0, 0, p, 0, 0))
     in_specs = [
         pl.BlockSpec((1, times, norb), lambda p, t, c: (first + p, 0, 0)),
-        blocks,
-        blocks,
+        brought,
+        brought,
         pl.BlockSpec((1, 1, blk, blk), lambda p, t, c: (t, first + p, 0, 0)),
     ]
-    operands = [core, factors, mine, other, screened]
     if carried is not None:
-        in_specs.append(pl.BlockSpec(carried.shape, lambda p, t, c: (0, 0, 0)))
-        operands.append(carried)
+        operands.append(in_hbm(carried))
+        in_specs.append(pl.BlockSpec(memory_space=pltpu.HBM))
     return pl.pallas_call(
         kernel,
         grid_spec=pltpu.PrefetchScalarGridSpec(
             num_scalar_prefetch=1,
             grid=(pairs, times),
             in_specs=in_specs,
-            out_specs=pl.BlockSpec(out_shape.shape, lambda p, t, c: (0,) * ends),
+            out_specs=out_spec,
             scratch_shapes=[
                 pltpu.VMEM((blk, norb), jnp.bfloat16),
                 pltpu.VMEM((blk, norb), jnp.bfloat16),
                 pltpu.VMEM((norb, blk), jnp.bfloat16),
                 pltpu.VMEM((blk, norb), jnp.bfloat16),
-                pltpu.VMEM((times, norb, norb), jnp.float32),
+                pltpu.VMEM(sums, jnp.float32),
+                pltpu.SemaphoreType.DMA((times,)),
             ],
         ),
         out_shape=out_shape,
         compiler_params=pltpu.CompilerParams(
-            vmem_limit_bytes=48 << 20, dimension_semantics=("arbitrary", "arbitrary")
+            vmem_limit_bytes=32 << 20, dimension_semantics=("arbitrary", "arbitrary")
         ),
     )(*operands)
 
@@ -167,7 +200,7 @@
         shape = (2, owners, 2 * pairs, rows, cols)
         last = first + pairs == pair_local
         total = pair_sums(
-            core, factors, mine.reshape(shape), other.reshape(shape), screened, first, pairs, total, last
+            core, factors, mine.reshape(shape), other.reshape(shape), screened, first, total, last
         )
     shares = lax.all_to_all(total, PAIR, 0, 0, tiled=True)
     return jnp.sum(shares.astype(jnp.float32), axis=0)

time: 152 us -> 153 us (level)
  blocking collectives: 39.4 us -> 112 us
  waiting for transfers between devices: 50.8 us -> 0.01 us
  starting transfers between devices: 13.8 us -> 0.01 us
  Pallas kernels: 42.7 us -> 37.7 us
    all_to_all x0 -> x2, blocking collectives: none -> 73.1 us  [shards(): mine = lax.all_to_all(picked, SAME_CORE, 0, 0, tiled=True)]
    all_to_all x2 -> x0, waiting for transfers between devices: 50.8 us -> none  [shards(): mine = lax.all_to_all(picked, SAME_CORE, 0, 0, tiled=True)]
    all_to_all x2 -> x0, starting transfers between devices: 13.7 us -> none  [shards(): mine = lax.all_to_all(picked, SAME_CORE, 0, 0, tiled=True)]
    pallas_call x2, Pallas kernels: 9.85 us -> 4.71 us  [picked_for(): pl.pallas_call(kernel, grid_spec=pltpu.PrefetchScalarGridSpec(num_scalar_...]
  transfers between devices with their start and end apart: 4 -> 2, of which waited for: 2 -> 0; matrix products, arithmetic and copies ran while one was open for 0% -> 0% of each run, Pallas kernels for 14% -> 17%
where the time goes in v2:
time: 153 us
  blocking collectives  112 us (73%)
  Pallas kernels  37.7 us (25%)
  other arithmetic  2.64 us (2%)
    all_to_all x2, blocking collectives, shards(): mine = lax.all_to_all(picked, SAME_CORE, 0, 0, tiled=True)  73.1 us
    pallas_call x2, Pallas kernels, pair_sums(): pl.pallas_call(kernel, grid_spec=pltpu.PrefetchScalarGridSpec(num_scalar_...  33 us
    all_to_all x1, blocking collectives, shards(): shares = lax.all_to_all(total, PAIR, 0, 0, tiled=True)  20.8 us
    all_to_all x1, blocking collectives, shards(): slices = lax.all_to_all(sent, PAIR, 0, 0, tiled=True)  18 us
    pallas_call x2, Pallas kernels, picked_for(): pl.pallas_call(kernel, grid_spec=pltpu.PrefetchScalarGridSpec(num_scalar_...  4.71 us
  transfers between devices with their start and end apart: 2, of which 0 were waited for; matrix products, arithmetic and copies ran while one was open for 0% of the time, Pallas kernels for 17%

profile of v2, /device:TPU:0, one launch (start us, length us, event | category | flops | bytes accessed | tf_op | source)
XLA Modules:
  0.0 152.6 jit_solution(903049971977705769)
XLA Ops:
  0.0 0.7 convert_element_type.27
  0.7 0.1 copy.6
  0.8 0.1 convert_element_type.28
  0.9 1.0 pad_maximum_fusion
  1.9 18.0 %all_to_all.20.slices_ref = bf16[32,40,128]{2,1,0:T(8,128)(2,1)S(1)} all-to-all(bf16[32,40,128]{2,1,0:T(8,128)(2,1)S(1)} %pad_maximum_fusion), channel_id=1, replica_groups=mesh['zh'=2,'core'=2,'zl'=2,'y'=4,'x'=4] {'zl','y','x'}, dimensions={0} | all-to-all | bytes 655360 | tf_op jit(solution)/shard_map/all_to_all | solution.py:182
  20.0 2.8 %shard_map.47 = bf16[2,32,6,32,128]{4,3,2,1,0:T(8,128)(2,1)} custom-call(s32[32,8]{1,0:T(8,128)S(1)} %bitcast.12, bf16[32,40,128]{2,1,0:T(8,128)(2,1)S(1)} %all_to_all.20.slices_ref), custom_call_target="tpu_custom_call" | custom-call | tf_op jit(solution)/shard_map/pallas_call | solution.py:38
  22.8 47.8 %all_to_all.21 = bf16[64,6,32,128]{3,2,1,0:T(8,128)(2,1)S(1)} all-to-all(bf16[64,6,32,128]{3,2,1,0:T(8,128)(2,1)} %bitcast.14), channel_id=1, replica_groups=mesh['zh'=2,'core'=2,'zl'=2,'y'=4,'x'=4] {'zh','zl','y','x'}, dimensions={0} | all-to-all | bytes 6291456 | tf_op jit(solution)/shard_map/all_to_all | solution.py:198
  70.6 0.0 copy-start
  70.6 0.0 copy-start.1
  70.6 0.0 collective-permute-start.1
  70.6 1.9 %shard_map.46 = bf16[2,32,2,32,128]{4,3,2,1,0:T(8,128)(2,1)} custom-call(s32[32,8]{1,0:T(8,128)S(1)} %bitcast.13, bf16[32,40,128]{2,1,0:T(8,128)(2,1)S(1)} %all_to_all.20.slices_ref), custom_call_target="tpu_custom_call" | custom-call | tf_op jit(solution)/shard_map/pallas_call | solution.py:38
  72.5 25.3 %all_to_all.22 = bf16[64,2,32,128]{3,2,1,0:T(8,128)(2,1)} all-to-all(bf16[64,2,32,128]{3,2,1,0:T(8,128)(2,1)} %bitcast.15), channel_id=1, replica_groups=mesh['zh'=2,'core'=2,'zl'=2,'y'=4,'x'=4] {'zh','zl','y','x'}, dimensions={0} | all-to-all | bytes 2097152 | tf_op jit(solution)/shard_map/all_to_all | solution.py:198
  97.8 0.0 collective-permute-start
  97.8 0.0 copy-done
  97.8 0.0 copy-done.1
  97.8 0.1 exponential_multiply_fusion
  97.9 0.1 broadcast_multiply_fusion.fac
  98.0 0.0 collective-permute-done.1
  98.0 23.4 %shard_map.48.refs_0_ = f32[2,512,512]{2,1,0:T(8,128)} custom-call(s32[1]{0:T(128)} %bitcast.core_ref, f32[4,2,512]{2,1,0:T(2,128)S(1)} %broadcast_multiply_fusion.fac, bf16[2,32,6,32,128]{4,3,2,1,0:T(8,128)(2,1)S(1)} %bitcast.11, bf16[2,32,6,32,128]{4,3,2,1,0:T(8,128)(2,1)} %bitcast.9.other_ref, bf16[2,4,1024,1024]{3,2,1,0:T(8,128)(2,1)} %tile.3), custom_call_target="tpu_custom_call" | custom-call | tf_op jit(solution)/shard_map/pallas_call | solution.py:143
  121.4 0.0 collective-permute-done
  121.4 9.6 %shard_map.49 = bf16[32,2,16,512]{3,2,1,0:T(8,128)(2,1)S(1)} custom-call(s32[1]{0:T(128)} %bitcast.core_ref, f32[4,2,512]{2,1,0:T(2,128)S(1)} %broadcast_multiply_fusion.fac, bf16[2,32,2,32,128]{4,3,2,1,0:T(8,128)(2,1)} %bitcast.5.mine_ref, bf16[2,32,2,32,128]{4,3,2,1,0:T(8,128)(2,1)} %bitcast.6.other_ref, bf16[2,4,1024,1024]{3,2,1,0:T(8,128)(2,1)} %tile.3, ...), custom_call_target="tpu_custom_call" | custom-call | tf_op jit(solution)/shard_map/pallas_call | solution.py:143
  131.0 20.8 %all_to_all.23 = bf16[32,2,16,512]{3,2,1,0:T(8,128)(2,1)S(1)} all-to-all(bf16[32,2,16,512]{3,2,1,0:T(8,128)(2,1)S(1)} %shard_map.49), channel_id=1, replica_groups=mesh['zh'=2,'core'=2,'zl'=2,'y'=4,'x'=4] {'zl','y','x'}, dimensions={0} | all-to-all | bytes 2097152 | tf_op jit(solution)/shard_map/all_to_all | solution.py:205
  151.8 0.8 convert_reduce_fusion
  (7 shorter events, 0.1 us)
Async XLA Ops:
  70.6 27.2 %copy-start = (f32[512]{0:T(512)S(1)}, f32[512]{0:T(512)}, u32[]{:S(2)}) copy-start(f32[512]{0:T(512)} %param.7) | copy-start | bytes 6148
  70.6 27.2 %copy-start.1 = (s32[4,2]{0,1:T(2,128)S(1)}, s32[4,2]{0,1:T(2,128)}, u32[]{:S(2)}) copy-start(s32[4,2]{0,1:T(2,128)} %param.9) | copy-start | bytes 100
  70.6 27.4 %collective-permute-start.1 = (bf16[64,6,32,128]{3,2,1,0:T(8,128)(2,1)S(1)}, bf16[64,6,32,128]{3,2,1,0:T(8,128)(2,1)}, u32[]{:S(2)}, u32[]{:S(2)}) collective-permute-start(bf16[64,6,32,128]{3,2,1,0:T(8,128)(2,1)S(1)} %all_to_all.21), channel_id=1, source_target_pairs={{0,32},{32,0},{1,33},{33,1},{2,34},{34,2},{3,35},{35,3},{4,36},{36... | collective-permute-start | bytes 9437192 | tf_op jit(solution)/shard_map/ppermute | solution.py:199
  97.8 23.6 %collective-permute-start = (bf16[64,2,32,128]{3,2,1,0:T(8,128)(2,1)}, bf16[64,2,32,128]{3,2,1,0:T(8,128)(2,1)}, u32[]{:S(2)}, u32[]{:S(2)}) collective-permute-start(bf16[64,2,32,128]{3,2,1,0:T(8,128)(2,1)} %all_to_all.22), channel_id=1, source_target_pairs={{0,32},{32,0},{1,33},{33,1},{2,34},{34,2},{3,35},{35,3},{4,36},{36... | collective-permute-start | bytes 3145736 | tf_op jit(solution)/shard_map/ppermute | solution.py:199

commit v3 on v2

v3 whole, which is shorter than its diff:
```python
import jax
import jax.numpy as jnp
from jax import lax
from jax.experimental import pallas as pl
from jax.experimental.pallas import tpu as pltpu
from jax.sharding import Mesh
from jax.sharding import PartitionSpec as P

NOCC = 128
PAIR = ("zl", "y", "x")
SAME_CORE = ("zh", "zl", "y", "x")
INDEX_ROWS = 8
FIRST = ((0, 1, 2), (3, 1, 2))


def in_hbm(array):
    return pltpu.with_memory_space_constraint(array, pltpu.HBM)


def picked_for(wants, slices):
    owners, rows, cols = slices.shape[0], slices.shape[1] - INDEX_ROWS, slices.shape[2]
    count = 2 * len(FIRST[0])
    per_step = 4

    def kernel(wants_ref, slices_ref, out_ref, sent):
        def some(i, unused):
            for d in range(per_step):
                for half in range(2):
                    for k in range(count):
                        block = wants_ref[i * per_step + d, 2 * FIRST[half][k // 2] + k % 2]
                        piece = slices_ref.at[block, pl.ds(0, rows), :]
                        at = out_ref.at[half, i * per_step + d, k]
                        pltpu.make_async_copy(piece, at, sent).start()
            return unused

        lax.fori_loop(0, owners // per_step, some, 0)
        pltpu.make_async_copy(out_ref, out_ref, sent).wait()

    return pl.pallas_call(
        kernel,
        grid_spec=pltpu.PrefetchScalarGridSpec(
            num_scalar_prefetch=1,
            grid=(1,),
            in_specs=[pl.BlockSpec(memory_space=pltpu.VMEM)],
            out_specs=pl.BlockSpec(memory_space=pltpu.HBM),
            scratch_shapes=[pltpu.SemaphoreType.DMA(())],
        ),
        out_shape=pltpu.HBM((2, owners, count, rows, cols), slices.dtype),
        compiler_params=pltpu.CompilerParams(vmem_limit_bytes=16 << 20),
    )(wants, slices)


def pair_sums(where, factors, mine, other, screened, carried):
    _, slots, blocks, rows, cols = mine.shape
    pairs = blocks // 2
    times, _, blk, _ = screened.shape
    norb = factors.shape[-1]
    strip = 256
    last = carried is not None

    def kernel(where_ref, fac, mine_ref, other_ref, screened_ref, *refs):
        start = None
        if last:
            start, *refs = refs
        out, left, right, inner, tiles, acc, got, seen, moved = refs
        p = pl.program_id(0)
        slot = lax.rem(p, 2)
        own = where_ref[0]

        def at_first(do):
            do() if pairs == 1 else pl.when(p == 0)(do)

        def at_last(do):
            do() if pairs == 1 else pl.when(p == pairs - 1)(do)

        def bring(q, to):
            for source, side in ((mine_ref, own), (other_ref, 1 - own)):
                for half in range(2):
                    at = pl.multiple_of((half * 2 + side) * cols, cols)
                    for b, target in enumerate((left, right)):
                        pltpu.make_async_copy(
                            source.at[half, :, 2 * q + b],
                            target.at[to, :, :, pl.ds(at, cols)],
                            got.at[b, to],
                        ).start()
            for t in range(times):
                tile(q, t, to).start()

        def tile(q, t, to):
            return pltpu.make_async_copy(
                screened_ref.at[t, where_ref[1 + q]], tiles.at[to, t], seen.at[to, t]
            )

        @at_first
        def _():
            bring(0, 0)
            if last:
                pltpu.make_async_copy(start, acc, moved.at[0]).start()
            else:
                acc[...] = jnp.zeros(acc.shape, acc.dtype)

        if pairs > 1:

            @pl.when(p + 1 < pairs)
            def _():
                bring(p + 1, 1 - slot)

        for b, target in enumerate((left, right)):
            pltpu.make_async_copy(target.at[slot], target.at[slot], got.at[b, slot]).wait()
        left_side = left[slot].reshape(blk, norb)
        right_side = right[slot].reshape(blk, norb)
        for t in range(times):
            tile(p, t, slot).wait()
            scale = fac[0, t : t + 1, :]
            for s in range(blk // strip):
                part = slice(s * strip, (s + 1) * strip)
                scaled = (left_side[part, :].astype(jnp.float32) * scale).astype(jnp.bfloat16)
                green = lax.dot_general(
                    scaled, right_side, (((1,), (1,)), ((), ())), preferred_element_type=jnp.float32
                )
                product = (green * tiles[slot, t, part, :].astype(jnp.float32)).astype(jnp.bfloat16)
                inner[t, part, :] = jnp.dot(
                    product, right_side, preferred_element_type=jnp.float32
                ).astype(jnp.bfloat16)
            if last and t == 0:

                @at_first
                def _():
                    pltpu.make_async_copy(start, acc, moved.at[0]).wait()

            acc[t] += lax.dot_general(
                left_side, inner[t], (((0,), (0,)), ((), ())), preferred_element_type=jnp.float32
            )

        @at_last
        def _():
            if last:
                for t in range(times):
                    total = acc[t]
                    both = (total + total.T).astype(out.dtype)
                    out[:, t] = both.reshape(out.shape[0], out.shape[2], norb)
            else:
                copies = [
                    pltpu.make_async_copy(acc.at[t], out.at[t], moved.at[t]) for t in range(times)
                ]
                for copy in copies:
                    copy.start()
                for copy in copies:
                    copy.wait()

    sums = (times, norb, norb)
    outside = pl.BlockSpec(memory_space=pltpu.HBM)
    anywhere = pl.BlockSpec(memory_space=pl.ANY)
    if last:
        out_shape = jax.ShapeDtypeStruct((slots, times, norb // slots, norb), jnp.bfloat16)
        out_spec = pl.BlockSpec(out_shape.shape, lambda p, c: (0, 0, 0, 0))
    else:
        out_shape = pltpu.HBM(sums, jnp.float32)
        out_spec = outside
    operands = [where, factors, mine, other, in_hbm(screened)]
    if last:
        operands.append(in_hbm(carried))
    return pl.pallas_call(
        kernel,
        grid_spec=pltpu.PrefetchScalarGridSpec(
            num_scalar_prefetch=1,
            grid=(pairs,),
            in_specs=[pl.BlockSpec((1, times, norb), lambda p, c: (c[1 + p], 0, 0))]
            + [anywhere] * 2
            + [outside] * (len(operands) - 4),
            out_specs=out_spec,
            scratch_shapes=[
                pltpu.VMEM((2, slots, rows, norb), jnp.bfloat16),
                pltpu.VMEM((2, slots, rows, norb), jnp.bfloat16),
                pltpu.VMEM((times, blk, norb), jnp.bfloat16),
                pltpu.VMEM((2, times, blk, blk), jnp.bfloat16),
                pltpu.VMEM(sums, jnp.float32),
                pltpu.SemaphoreType.DMA((2, 2)),
                pltpu.SemaphoreType.DMA((2, times)),
                pltpu.SemaphoreType.DMA((times,)),
            ],
        ),
        out_shape=out_shape,
        compiler_params=pltpu.CompilerParams(
            vmem_limit_bytes=40 << 20, dimension_semantics=("arbitrary",)
        ),
    )(*operands)


def shards(orbitals, level_gap, screened, pair_blocks):
    owners = lax.axis_size(PAIR)
    cols = orbitals.shape[1]
    rows = orbitals.shape[0] // owners
    time_local, pair_local = screened.shape[:2]
    norb = level_gap.shape[0]

    asked = jnp.zeros((INDEX_ROWS, cols), jnp.bfloat16)
    asked = asked.at[0, : 2 * pair_local].set(pair_blocks.reshape(-1).astype(jnp.bfloat16))
    sent = jnp.concatenate(
        [
            orbitals.reshape(owners, rows, cols),
            jnp.broadcast_to(asked, (owners, INDEX_ROWS, cols)),
        ],
        axis=1,
    )
    slices = lax.all_to_all(sent, PAIR, 0, 0, tiled=True)
    wants = slices[:, rows, : 2 * pair_local].astype(jnp.int32)

    half = lax.axis_index("zh")
    core = lax.axis_index("core")
    first = jnp.where(half == 0, FIRST[0][0], FIRST[1][0])
    final = jnp.where(half == 0, FIRST[1][0], FIRST[0][0])
    opening = jnp.stack([core, first, FIRST[0][1], FIRST[0][2]]).astype(jnp.int32)
    closing = jnp.stack([core, final]).astype(jnp.int32)
    swap = [(0, 1), (1, 0)]
    picked = picked_for(wants, slices).reshape(2 * owners, -1, rows, cols)
    mine = lax.all_to_all(picked, SAME_CORE, 0, 0, tiled=True)
    moments = ((half * 2 + core) * time_local + jnp.arange(time_local)).astype(jnp.float32)
    tau = 6.0 * (moments + 0.5) / (time_local * lax.axis_size(("zh", "core")))
    signs = jnp.where(jnp.arange(norb) < NOCC, 1.0, -1.0).astype(jnp.float32)
    weights = jnp.where(pair_blocks[:, 0] == pair_blocks[:, 1], 0.5, 1.0).astype(jnp.float32)
    factors = signs[None, :] * jnp.exp(-level_gap[None, :] * tau[:, None])
    factors = weights[:, None, None] * factors[None]
    other = lax.ppermute(mine, "core", swap)
    traded = lax.ppermute(mine[:, :2], "zh", swap)
    shape = (2, owners, -1, rows, cols)
    total = pair_sums(opening, factors, mine.reshape(shape), other.reshape(shape), screened, None)
    twin = lax.ppermute(traded, "core", swap)
    total = pair_sums(closing, factors, traded.reshape(shape), twin.reshape(shape), screened, total)
    shares = lax.all_to_all(total, PAIR, 0, 0, tiled=True)
    return jnp.sum(shares.astype(jnp.float32), axis=0)


def solution(mesh):
    fine = Mesh(mesh.devices.reshape(2, 2, 2, 4, 4), ("zh", "core", "zl", "y", "x"))
    tm = ("zh", "core")
    placed = (P(PAIR, tm), P(), P(tm, PAIR, None, None), P(PAIR, None))
    return jax.shard_map(
        shards, mesh=fine, in_specs=placed, out_specs=P(tm, PAIR, None), check_vma=False
    )
```

time: 153 us -> 153 us (level)
  waiting for transfers between devices: 0.01 us -> 26.8 us
  blocking collectives: 112 us -> 86.6 us
  Pallas kernels: 37.7 us -> 34.9 us
    ppermute x2 -> x3, waiting for transfers between devices: 0.01 us -> 26.8 us  [the longest x1 26.8 us: shards(): traded = lax.ppermute(mine[:, :2], 'zh', swap)]
    all_to_all x2 -> x1, blocking collectives: 73.1 us -> 47.8 us  [shards(): mine = lax.all_to_all(picked, SAME_CORE, 0, 0, tiled=True)]
    pallas_call x2 -> x1, Pallas kernels: 4.71 us -> 2.84 us  [picked_for(): pl.pallas_call(kernel, grid_spec=pltpu.PrefetchScalarGridSpec(num_scalar_...]
  transfers between devices with their start and end apart: 2 -> 3, of which waited for: 0 -> 1; matrix products, arithmetic and copies ran while one was open for 0% -> 1% of each run, Pallas kernels for 17% -> 15%
where the time goes in v3:
time: 153 us
  blocking collectives  86.6 us (57%)
  Pallas kernels  34.9 us (23%)
  waiting for transfers between devices  26.8 us (18%)
  other arithmetic  2.79 us (2%)
    all_to_all x1, blocking collectives, shards(): mine = lax.all_to_all(picked, SAME_CORE, 0, 0, tiled=True)  47.8 us
    pallas_call x2, Pallas kernels, pair_sums(): pl.pallas_call(kernel, grid_spec=pltpu.PrefetchScalarGridSpec(num_scalar_...  32.1 us
    ppermute x1, waiting for transfers between devices, shards(): traded = lax.ppermute(mine[:, :2], 'zh', swap)  26.8 us
    all_to_all x1, blocking collectives, shards(): shares = lax.all_to_all(total, PAIR, 0, 0, tiled=True)  20.8 us
    all_to_all x1, blocking collectives, shards(): slices = lax.all_to_all(sent, PAIR, 0, 0, tiled=True)  18 us
  transfers between devices with their start and end apart: 3, of which 1 were waited for; matrix products, arithmetic and copies ran while one was open for 1% of the time, Pallas kernels for 15%

profile of v3, /device:TPU:0, one launch (start us, length us, event | category | flops | bytes accessed | tf_op | source)
XLA Modules:
  0.0 153.1 jit_solution(13886905352229823147)
XLA Ops:
  0.0 0.7 convert_element_type.27
  0.7 0.1 copy.6
  0.8 0.1 convert_element_type.28
  0.9 1.0 pad_maximum_fusion
  1.9 18.0 %all_to_all.15.slices_ref = bf16[32,40,128]{2,1,0:T(8,128)(2,1)S(1)} all-to-all(bf16[32,40,128]{2,1,0:T(8,128)(2,1)S(1)} %pad_maximum_fusion), channel_id=1, replica_groups=mesh['zh'=2,'core'=2,'zl'=2,'y'=4,'x'=4] {'zl','y','x'}, dimensions={0} | all-to-all | bytes 655360 | tf_op jit(solution)/shard_map/all_to_all | solution.py:206
  20.0 2.8 %shard_map.46 = bf16[2,32,6,32,128]{4,3,2,1,0:T(8,128)(2,1)} custom-call(s32[32,8]{1,0:T(8,128)S(1)} %bitcast.13, bf16[32,40,128]{2,1,0:T(8,128)(2,1)S(1)} %all_to_all.15.slices_ref), custom_call_target="tpu_custom_call" | custom-call | tf_op jit(solution)/shard_map/pallas_call | solution.py:39
  22.8 0.0 copy-start
  22.8 0.0 copy-start.1
  22.8 47.8 %all_to_all.16 = bf16[64,6,32,128]{3,2,1,0:T(8,128)(2,1)S(1)} all-to-all(bf16[64,6,32,128]{3,2,1,0:T(8,128)(2,1)} %bitcast.14), channel_id=1, replica_groups=mesh['zh'=2,'core'=2,'zl'=2,'y'=4,'x'=4] {'zh','zl','y','x'}, dimensions={0} | all-to-all | bytes 6291456 | tf_op jit(solution)/shard_map/all_to_all | solution.py:217
  70.6 0.0 collective-permute-start.2
  70.6 1.0 slice.33
  71.7 0.6 collective-permute-start
  72.3 26.8 %collective-permute-done = bf16[64,2,32,128]{3,2,1,0:T(8,128)(2,1)} collective-permute-done((bf16[64,2,32,128]{3,2,1,0:T(8,128)(2,1)}, bf16[64,2,32,128]{3,2,1,0:T(8,128)(2,1)}, u32[]{:S(2)}, u32[]{:S(2)}) %collective-permute-start) | collective-permute-done | bytes 1048608 | tf_op jit(solution)/shard_map/ppermute | solution.py:225
  99.1 0.0 collective-permute-start.1
  99.1 0.0 copy-done
  99.1 0.1 pad_add_fusion.where_ref
  99.2 0.1 pad_add_fusion.1.where_ref
  99.3 0.0 copy-done.1
  99.3 0.1 exponential_multiply_fusion
  99.4 0.1 broadcast_multiply_fusion.fac
  99.4 0.0 collective-permute-done.2
  99.4 22.2 %shard_map.47.refs_0_ = f32[2,512,512]{2,1,0:T(8,128)} custom-call(s32[4]{0:T(128)S(1)} %pad_add_fusion.1.where_ref, f32[4,2,512]{2,1,0:T(2,128)S(1)} %broadcast_multiply_fusion.fac, bf16[2,32,6,32,128]{4,3,2,1,0:T(8,128)(2,1)S(1)} %bitcast.12, bf16[2,32,6,32,128]{4,3,2,1,0:T(8,128)(2,1)} %bitcast.10.other_ref, bf16[2,4,1024,1024]{3,2,1,0:T(8,128)(2,1)} %screened_ref.3), custom_call_target="tpu_custom_call" | custom-call | tf_op jit(solution)/shard_map/pallas_call | solution.py:163
  121.7 0.0 collective-permute-done.1
  121.7 9.8 %shard_map.48 = bf16[32,2,16,512]{3,2,1,0:T(8,128)(2,1)S(1)} custom-call(s32[2]{0:T(128)S(1)} %pad_add_fusion.where_ref, f32[4,2,512]{2,1,0:T(2,128)S(1)} %broadcast_multiply_fusion.fac, bf16[2,32,2,32,128]{4,3,2,1,0:T(8,128)(2,1)} %bitcast.6.mine_ref, bf16[2,32,2,32,128]{4,3,2,1,0:T(8,128)(2,1)} %bitcast.7.other_ref, ...), custom_call_target="tpu_custom_call" | custom-call | tf_op jit(solution)/shard_map/pallas_call | solution.py:163
  131.5 20.8 %all_to_all.17 = bf16[32,2,16,512]{3,2,1,0:T(8,128)(2,1)S(1)} all-to-all(bf16[32,2,16,512]{3,2,1,0:T(8,128)(2,1)S(1)} %shard_map.48), channel_id=1, replica_groups=mesh['zh'=2,'core'=2,'zl'=2,'y'=4,'x'=4] {'zl','y','x'}, dimensions={0} | all-to-all | bytes 2097152 | tf_op jit(solution)/shard_map/all_to_all | solution.py:230
  152.3 0.8 convert_reduce_fusion
  (7 shorter events, 0.1 us)
Async XLA Ops:
  22.8 76.3 %copy-start = (f32[512]{0:T(512)S(1)}, f32[512]{0:T(512)}, u32[]{:S(2)}) copy-start(f32[512]{0:T(512)} %param.7) | copy-start | bytes 6148
  22.8 76.5 %copy-start.1 = (s32[4,2]{0,1:T(2,128)S(1)}, s32[4,2]{0,1:T(2,128)}, u32[]{:S(2)}) copy-start(s32[4,2]{0,1:T(2,128)} %param.9) | copy-start | bytes 100
  70.6 28.8 %collective-permute-start.2 = (bf16[64,6,32,128]{3,2,1,0:T(8,128)(2,1)S(1)}, bf16[64,6,32,128]{3,2,1,0:T(8,128)(2,1)}, u32[]{:S(2)}, u32[]{:S(2)}) collective-permute-start(bf16[64,6,32,128]{3,2,1,0:T(8,128)(2,1)S(1)} %all_to_all.16), channel_id=1, source_target_pairs={{0,32},{32,0},{1,33},{33,1},{2,34},{34,2},{3,35},{35,3},{4,36},{36... | collective-permute-start | bytes 9437192 | tf_op jit(solution)/shard_map/ppermute | solution.py:224
  71.7 27.4 %collective-permute-start = (bf16[64,2,32,128]{3,2,1,0:T(8,128)(2,1)}, bf16[64,2,32,128]{3,2,1,0:T(8,128)(2,1)}, u32[]{:S(2)}, u32[]{:S(2)}) collective-permute-start(bf16[64,2,32,128]{3,2,1,0:T(8,128)(2,1)} %slice.33), channel_id=1, source_target_pairs={{0,64},{64,0},{1,65},{65,1},{2,66},{66,2},{3,67},{67,3},{4,68},{68... | collective-permute-start | bytes 3145736 | tf_op jit(solution)/shard_map/ppermute | solution.py:225
  99.1 22.6 %collective-permute-start.1 = (bf16[64,2,32,128]{3,2,1,0:T(8,128)(2,1)}, bf16[64,2,32,128]{3,2,1,0:T(8,128)(2,1)}, u32[]{:S(2)}, u32[]{:S(2)}) collective-permute-start(bf16[64,2,32,128]{3,2,1,0:T(8,128)(2,1)} %collective-permute-done), channel_id=1, source_target_pairs={{0,32},{32,0},{1,33},{33,1},{2,34},{34,2},{3,35},{35,3},{4,36},{36... | collective-permute-start | bytes 3145736 | tf_op jit(solution)/shard_map/ppermute | solution.py:228

commit v4 on v3

--- a/solution.py
+++ b/solution.py
@@ -58,20 +58,14 @@
     strip = 256
     last = carried is not None
 
-    def kernel(where_ref, fac, mine_ref, other_ref, screened_ref, *refs):
-        start = None
+    def kernel(where_ref, fac, mine_ref, other_ref, *refs):
         if last:
-            start, *refs = refs
-        out, left, right, inner, tiles, acc, got, seen, moved = refs
+            start, tiles, out, left, right, inner, got = refs
+        else:
+            screened_ref, out, ahead, left, right, inner, tiles, got, seen, moved = refs
         p = pl.program_id(0)
-        slot = lax.rem(p, 2)
+        slot = 0 if last else lax.rem(p, 2)
         own = where_ref[0]
-
-        def at_first(do):
-            do() if pairs == 1 else pl.when(p == 0)(do)
-
-        def at_last(do):
-            do() if pairs == 1 else pl.when(p == pairs - 1)(do)
 
         def bring(q, to):
             for source, side in ((mine_ref, own), (other_ref, 1 - own)):
@@ -83,23 +77,30 @@
                             target.at[to, :, :, pl.ds(at, cols)],
                             got.at[b, to],
                         ).start()
-            for t in range(times):
-                tile(q, t, to).start()
+            if not last:
+                for t in range(times):
+                    tile(q, t, to).start()
 
         def tile(q, t, to):
             return pltpu.make_async_copy(
                 screened_ref.at[t, where_ref[1 + q]], tiles.at[to, t], seen.at[to, t]
             )
 
-        @at_first
-        def _():
+        def later(t):
+            return pltpu.make_async_copy(
+                screened_ref.at[t, where_ref[1 + pairs]], ahead.at[t], moved.at[t]
+            )
+
+        if last:
             bring(0, 0)
-            if last:
-                pltpu.make_async_copy(start, acc, moved.at[0]).start()
-            else:
-                acc[...] = jnp.zeros(acc.shape, acc.dtype)
-
-        if pairs > 1:
+        else:
+
+            @pl.when(p == 0)
+            def _():
+                bring(0, 0)
+                for t in range(times):
+                    later(t).start()
+                out[...] = jnp.zeros(out.shape, out.dtype)
 
             @pl.when(p + 1 < pairs)
             def _():
@@ -110,7 +111,8 @@
         left_side = left[slot].reshape(blk, norb)
         right_side = right[slot].reshape(blk, norb)
         for t in range(times):
-            tile(p, t, slot).wait()
+            if not last:
+                tile(p, t, slot).wait()
             scale = fac[0, t : t + 1, :]
             for s in range(blk // strip):
                 part = slice(s * strip, (s + 1) * strip)
@@ -118,73 +120,74 @@
                 green = lax.dot_general(
                     scaled, right_side, (((1,), (1,)), ((), ())), preferred_element_type=jnp.float32
                 )
-                product = (green * tiles[slot, t, part, :].astype(jnp.float32)).astype(jnp.bfloat16)
+                held = tiles[t, part, :] if last else tiles[slot, t, part, :]
+                product = (green * held.astype(jnp.float32)).astype(jnp.bfloat16)
                 inner[t, part, :] = jnp.dot(
                     product, right_side, preferred_element_type=jnp.float32
                 ).astype(jnp.bfloat16)
-            if last and t == 0:
-
-                @at_first
-                def _():
-                    pltpu.make_async_copy(start, acc, moved.at[0]).wait()
-
-            acc[t] += lax.dot_general(
+            added = lax.dot_general(
                 left_side, inner[t], (((0,), (0,)), ((), ())), preferred_element_type=jnp.float32
             )
-
-        @at_last
-        def _():
             if last:
+                total = start[t] + added
+                both = (total + total.T).astype(out.dtype)
+                out[:, t] = both.reshape(out.shape[0], out.shape[2], norb)
+            else:
+                out[t] += added
+
+        if not last:
+
+            @pl.when(p == pairs - 1)
+            def _():
                 for t in range(times):
-                    total = acc[t]
-                    both = (total + total.T).astype(out.dtype)
-                    out[:, t] = both.reshape(out.shape[0], out.shape[2], norb)
-            else:
-                copies = [
-                    pltpu.make_async_copy(acc.at[t], out.at[t], moved.at[t]) for t in range(times)
-                ]
-                for copy in copies:
-                    copy.start()
-                for copy in copies:
-                    copy.wait()
+                    later(t).wait()
 
     sums = (times, norb, norb)
-    outside = pl.BlockSpec(memory_space=pltpu.HBM)
+    here = pl.BlockSpec(memory_space=pltpu.VMEM)
     anywhere = pl.BlockSpec(memory_space=pl.ANY)
+    buffers = 1 if last else 2
+    scratch = [
+        pltpu.VMEM((buffers, slots, rows, norb), jnp.bfloat16),
+        pltpu.VMEM((buffers, slots, rows, norb), jnp.bfloat16),
+        pltpu.VMEM((times, blk, norb), jnp.bfloat16),
+    ]
     if last:
+        operands, specs = list(carried), [here, here]
+        scratch += [pltpu.SemaphoreType.DMA((2, buffers))]
         out_shape = jax.ShapeDtypeStruct((slots, times, norb // slots, norb), jnp.bfloat16)
-        out_spec = pl.BlockSpec(out_shape.shape, lambda p, c: (0, 0, 0, 0))
+        out_specs = here
     else:
-        out_shape = pltpu.HBM(sums, jnp.float32)
-        out_spec = outside
-    operands = [where, factors, mine, other, in_hbm(screened)]
-    if last:
-        operands.append(in_hbm(carried))
+        operands, specs = [in_hbm(screened)], [pl.BlockSpec(memory_space=pltpu.HBM)]
+        scratch += [
+            pltpu.VMEM((buffers, times, blk, blk), jnp.bfloat16),
+            pltpu.SemaphoreType.DMA((2, buffers)),
+            pltpu.SemaphoreType.DMA((buffers, times)),
+            pltpu.SemaphoreType.DMA((times,)),
+        ]
+        out_shape = (
+            jax.ShapeDtypeStruct(sums, jnp.float32),
+            jax.ShapeDtypeStruct((times, blk, blk), jnp.bfloat16),
+        )
+        out_specs = (here, here)
     return pl.pallas_call(
         kernel,
         grid_spec=pltpu.PrefetchScalarGridSpec(
             num_scalar_prefetch=1,
             grid=(pairs,),
-            in_specs=[pl.BlockSpec((1, times, norb), lambda p, c: (c[1 + p], 0, 0))]
-            + [anywhere] * 2
-            + [outside] * (len(operands) - 4),
-            out_specs=out_spec,
-            scratch_shapes=[
-                pltpu.VMEM((2, slots, rows, norb), jnp.bfloat16),
-                pltpu.VMEM((2, slots, rows, norb), jnp.bfloat16),
-                pltpu.VMEM((times, blk, norb), jnp.bfloat16),
-                pltpu.VMEM((2, times, blk, blk), jnp.bfloat16),
-                pltpu.VMEM(sums, jnp.float32),
-                pltpu.SemaphoreType.DMA((2, 2)),
-                pltpu.SemaphoreType.DMA((2, times)),
-                pltpu.SemaphoreType.DMA((times,)),
-            ],
+            in_specs=[
+                pl.BlockSpec((1, times, norb), lambda p, c: (c[1 + p], 0, 0)),
+                anywhere,
+                anywhere,
+            ]
+            + specs,
+            out_specs=out_specs,
+            scratch_shapes=scratch,
         ),
         out_shape=out_shape,
         compiler_params=pltpu.CompilerParams(
             vmem_limit_bytes=40 << 20, dimension_semantics=("arbitrary",)
         ),
-    )(*operands)
+    )(where, factors, mine, other, *operands)
 
 
 def shards(orbitals, level_gap, screened, pair_blocks):
@@ -210,7 +213,7 @@
     core = lax.axis_index("core")
     first = jnp.where(half == 0, FIRST[0][0], FIRST[1][0])
     final = jnp.where(half == 0, FIRST[1][0], FIRST[0][0])
-    opening = jnp.stack([core, first, FIRST[0][1], FIRST[0][2]]).astype(jnp.int32)
+    opening = jnp.stack([core, first, FIRST[0][1], FIRST[0][2], final]).astype(jnp.int32)
     closing = jnp.stack([core, final]).astype(jnp.int32)
     swap = [(0, 1), (1, 0)]
     picked = picked_for(wants, slices).reshape(2 * owners, -1, rows, cols)
@@ -224,9 +227,9 @@
     other = lax.ppermute(mine, "core", swap)
     traded = lax.ppermute(mine[:, :2], "zh", swap)
     shape = (2, owners, -1, rows, cols)
-    total = pair_sums(opening, factors, mine.reshape(shape), other.reshape(shape), screened, None)
+    kept = pair_sums(opening, factors, mine.reshape(shape), other.reshape(shape), screened, None)
     twin = lax.ppermute(traded, "core", swap)
-    total = pair_sums(closing, factors, traded.reshape(shape), twin.reshape(shape), screened, total)
+    total = pair_sums(closing, factors, traded.reshape(shape), twin.reshape(shape), screened, kept)
     shares = lax.all_to_all(total, PAIR, 0, 0, tiled=True)
     return jnp.sum(shares.astype(jnp.float32), axis=0)
 

time: 153 us -> 149 us (0.974)
  Pallas kernels: 34.9 us -> 31.9 us
    pallas_call x2, Pallas kernels: 32.1 us -> 29 us  [pair_sums(): pl.pallas_call(kernel, grid_spec=pltpu.PrefetchScalarGridSpec(num_scalar_...]
  transfers between devices with their start and end apart: 3 -> 3, of which waited for: 1 -> 1; matrix products, arithmetic and copies ran while one was open for 1% -> 0% of each run, Pallas kernels for 15% -> 14%
where the time goes in v4:
time: 149 us
  blocking collectives  86.6 us (58%)
  Pallas kernels  31.9 us (21%)
  waiting for transfers between devices  26.5 us (18%)
  other arithmetic  2.71 us (2%)
    all_to_all x1, blocking collectives, shards(): mine = lax.all_to_all(picked, SAME_CORE, 0, 0, tiled=True)  47.8 us
    pallas_call x2, Pallas kernels, pair_sums(): pl.pallas_call(kernel, grid_spec=pltpu.PrefetchScalarGridSpec(num_scalar_...  29 us
    ppermute x1, waiting for transfers between devices, shards(): traded = lax.ppermute(mine[:, :2], 'zh', swap)  26.5 us
    all_to_all x1, blocking collectives, shards(): shares = lax.all_to_all(total, PAIR, 0, 0, tiled=True)  20.8 us
    all_to_all x1, blocking collectives, shards(): slices = lax.all_to_all(sent, PAIR, 0, 0, tiled=True)  18 us
  transfers between devices with their start and end apart: 3, of which 1 were waited for; matrix products, arithmetic and copies ran while one was open for 0% of the time, Pallas kernels for 14%

profile of v4, /device:TPU:0, one launch (start us, length us, event | category | flops | bytes accessed | tf_op | source)
XLA Modules:
  0.0 148.9 jit_solution(16471997805299987442)
XLA Ops:
  0.0 0.7 convert_element_type.27
  0.7 0.1 copy.6
  0.8 0.1 convert_element_type.28
  0.9 1.0 pad_maximum_fusion
  1.9 18.0 %all_to_all.15.slices_ref = bf16[32,40,128]{2,1,0:T(8,128)(2,1)S(1)} all-to-all(bf16[32,40,128]{2,1,0:T(8,128)(2,1)S(1)} %pad_maximum_fusion), channel_id=1, replica_groups=mesh['zh'=2,'core'=2,'zl'=2,'y'=4,'x'=4] {'zl','y','x'}, dimensions={0} | all-to-all | bytes 655360 | tf_op jit(solution)/shard_map/all_to_all | solution.py:209
  20.0 2.8 %shard_map.46 = bf16[2,32,6,32,128]{4,3,2,1,0:T(8,128)(2,1)} custom-call(s32[32,8]{1,0:T(8,128)S(1)} %bitcast.13, bf16[32,40,128]{2,1,0:T(8,128)(2,1)S(1)} %all_to_all.15.slices_ref), custom_call_target="tpu_custom_call" | custom-call | tf_op jit(solution)/shard_map/pallas_call | solution.py:39
  22.8 0.0 copy-start
  22.8 0.0 copy-start.1
  22.8 47.8 %all_to_all.16 = bf16[64,6,32,128]{3,2,1,0:T(8,128)(2,1)S(1)} all-to-all(bf16[64,6,32,128]{3,2,1,0:T(8,128)(2,1)} %bitcast.14), channel_id=1, replica_groups=mesh['zh'=2,'core'=2,'zl'=2,'y'=4,'x'=4] {'zh','zl','y','x'}, dimensions={0} | all-to-all | bytes 6291456 | tf_op jit(solution)/shard_map/all_to_all | solution.py:220
  70.6 0.0 collective-permute-start.2
  70.6 0.1 slice.33
  70.7 0.7 collective-permute-start
  71.4 26.5 %collective-permute-done = bf16[64,2,32,128]{3,2,1,0:T(8,128)(2,1)} collective-permute-done((bf16[64,2,32,128]{3,2,1,0:T(8,128)(2,1)S(1)}, bf16[64,2,32,128]{3,2,1,0:T(8,128)(2,1)}, u32[]{:S(2)}, u32[]{:S(2)}) %collective-permute-start) | collective-permute-done | bytes 1048608 | tf_op jit(solution)/shard_map/ppermute | solution.py:228
  98.0 0.0 collective-permute-start.1
  98.0 0.0 copy-done
  98.0 0.1 stack.21.where_ref
  98.1 0.1 pad_add_fusion.where_ref
  98.2 0.0 copy-done.1
  98.2 0.1 exponential_multiply_fusion
  98.3 0.1 broadcast_multiply_fusion.fac
  98.3 0.0 collective-permute-done.2
  98.3 20.9 %shard_map.47 = (f32[2,512,512]{2,1,0:T(8,128)S(1)}, bf16[2,1024,1024]{2,1,0:T(8,128)(2,1)S(1)}) custom-call(s32[5]{0:T(128)S(1)} %stack.21.where_ref, f32[4,2,512]{2,1,0:T(2,128)S(1)} %broadcast_multiply_fusion.fac, bf16[2,32,6,32,128]{4,3,2,1,0:T(8,128)(2,1)S(1)} %bitcast.12, bf16[2,32,6,32,128]{4,3,2,1,0:T(8,128)(2,1)} %bitcast.10.other_ref, ...), custom_call_target="tpu_custom_call" | custom-call | tf_op jit(solution)/shard_map/pallas_call | solution.py:172
  119.2 0.0 collective-permute-done.1
  119.3 8.1 %shard_map.48 = bf16[32,2,16,512]{3,2,1,0:T(8,128)(2,1)S(1)} custom-call(s32[2]{0:T(128)S(1)} %pad_add_fusion.where_ref, f32[4,2,512]{2,1,0:T(2,128)S(1)} %broadcast_multiply_fusion.fac, bf16[2,32,2,32,128]{4,3,2,1,0:T(8,128)(2,1)} %bitcast.6.mine_ref, bf16[2,32,2,32,128]{4,3,2,1,0:T(8,128)(2,1)} %bitcast.7.other_ref, ...), custom_call_target="tpu_custom_call" | custom-call | tf_op jit(solution)/shard_map/pallas_call | solution.py:172
  127.4 20.8 %all_to_all.17 = bf16[32,2,16,512]{3,2,1,0:T(8,128)(2,1)S(1)} all-to-all(bf16[32,2,16,512]{3,2,1,0:T(8,128)(2,1)S(1)} %shard_map.48), channel_id=1, replica_groups=mesh['zh'=2,'core'=2,'zl'=2,'y'=4,'x'=4] {'zl','y','x'}, dimensions={0} | all-to-all | bytes 2097152 | tf_op jit(solution)/shard_map/all_to_all | solution.py:233
  148.2 0.8 convert_reduce_fusion
  (7 shorter events, 0.1 us)
Async XLA Ops:
  22.8 75.2 %copy-start = (f32[512]{0:T(512)S(1)}, f32[512]{0:T(512)}, u32[]{:S(2)}) copy-start(f32[512]{0:T(512)} %param.7) | copy-start | bytes 6148
  22.8 75.3 %copy-start.1 = (s32[4,2]{0,1:T(2,128)S(1)}, s32[4,2]{0,1:T(2,128)}, u32[]{:S(2)}) copy-start(s32[4,2]{0,1:T(2,128)} %param.9) | copy-start | bytes 100
  70.6 27.7 %collective-permute-start.2 = (bf16[64,6,32,128]{3,2,1,0:T(8,128)(2,1)S(1)}, bf16[64,6,32,128]{3,2,1,0:T(8,128)(2,1)}, u32[]{:S(2)}, u32[]{:S(2)}) collective-permute-start(bf16[64,6,32,128]{3,2,1,0:T(8,128)(2,1)S(1)} %all_to_all.16), channel_id=1, source_target_pairs={{0,32},{32,0},{1,33},{33,1},{2,34},{34,2},{3,35},{35,3},{4,36},{36... | collective-permute-start | bytes 9437192 | tf_op jit(solution)/shard_map/ppermute | solution.py:227
  70.7 27.3 %collective-permute-start = (bf16[64,2,32,128]{3,2,1,0:T(8,128)(2,1)S(1)}, bf16[64,2,32,128]{3,2,1,0:T(8,128)(2,1)}, u32[]{:S(2)}, u32[]{:S(2)}) collective-permute-start(bf16[64,2,32,128]{3,2,1,0:T(8,128)(2,1)S(1)} %slice.33), channel_id=1, source_target_pairs={{0,64},{64,0},{1,65},{65,1},{2,66},{66,2},{3,67},{67,3},{4,68},{68... | collective-permute-start | bytes 3145736 | tf_op jit(solution)/shard_map/ppermute | solution.py:228
  98.0 21.3 %collective-permute-start.1 = (bf16[64,2,32,128]{3,2,1,0:T(8,128)(2,1)}, bf16[64,2,32,128]{3,2,1,0:T(8,128)(2,1)}, u32[]{:S(2)}, u32[]{:S(2)}) collective-permute-start(bf16[64,2,32,128]{3,2,1,0:T(8,128)(2,1)} %collective-permute-done), channel_id=1, source_target_pairs={{0,32},{32,0},{1,33},{33,1},{2,34},{34,2},{3,35},{35,3},{4,36},{36... | collective-permute-start | bytes 3145736 | tf_op jit(solution)/shard_map/ppermute | solution.py:231

commit v5 on v4

--- a/solution.py
+++ b/solution.py
@@ -51,14 +51,16 @@
 
 
 def pair_sums(where, factors, mine, other, screened, carried):
-    _, slots, blocks, rows, cols = mine.shape
-    pairs = blocks // 2
+    _, slots, blocks, rows, cols = mine[0].shape
+    parts = len(mine)
+    pairs = blocks * parts // 2
     times, _, blk, _ = screened.shape
     norb = factors.shape[-1]
     strip = 256
     last = carried is not None
 
-    def kernel(where_ref, fac, mine_ref, other_ref, *refs):
+    def kernel(where_ref, fac, *refs):
+        mine_refs, other_refs, refs = refs[:parts], refs[parts : 2 * parts], refs[2 * parts :]
         if last:
             start, tiles, out, left, right, inner, got = refs
         else:
@@ -68,12 +70,12 @@
         own = where_ref[0]
 
         def bring(q, to):
-            for source, side in ((mine_ref, own), (other_ref, 1 - own)):
+            for sources, side in ((mine_refs, own), (other_refs, 1 - own)):
                 for half in range(2):
                     at = pl.multiple_of((half * 2 + side) * cols, cols)
                     for b, target in enumerate((left, right)):
                         pltpu.make_async_copy(
-                            source.at[half, :, 2 * q + b],
+                            sources[b % parts].at[half, :, (2 * q + b) // parts],
                             target.at[to, :, :, pl.ds(at, cols)],
                             got.at[b, to],
                         ).start()
@@ -176,9 +178,8 @@
             grid=(pairs,),
             in_specs=[
                 pl.BlockSpec((1, times, norb), lambda p, c: (c[1 + p], 0, 0)),
-                anywhere,
-                anywhere,
             ]
+            + [anywhere] * (2 * parts)
             + specs,
             out_specs=out_specs,
             scratch_shapes=scratch,
@@ -187,7 +188,7 @@
         compiler_params=pltpu.CompilerParams(
             vmem_limit_bytes=40 << 20, dimension_semantics=("arbitrary",)
         ),
-    )(where, factors, mine, other, *operands)
+    )(where, factors, *mine, *other, *operands)
 
 
 def shards(orbitals, level_gap, screened, pair_blocks):
@@ -225,11 +226,18 @@
     factors = signs[None, :] * jnp.exp(-level_gap[None, :] * tau[:, None])
     factors = weights[:, None, None] * factors[None]
     other = lax.ppermute(mine, "core", swap)
-    traded = lax.ppermute(mine[:, :2], "zh", swap)
+    traded, twins = [], []
+    for b in range(2):
+        traded.append(lax.ppermute(mine[:, b : b + 1], "zh", swap))
     shape = (2, owners, -1, rows, cols)
-    kept = pair_sums(opening, factors, mine.reshape(shape), other.reshape(shape), screened, None)
-    twin = lax.ppermute(traded, "core", swap)
-    total = pair_sums(closing, factors, traded.reshape(shape), twin.reshape(shape), screened, kept)
+    kept = pair_sums(
+        opening, factors, [mine.reshape(shape)], [other.reshape(shape)], screened, None
+    )
+    for b in range(2):
+        twins.append(lax.ppermute(traded[b], "core", swap))
+    traded = [part.reshape(shape) for part in traded]
+    twins = [part.reshape(shape) for part in twins]
+    total = pair_sums(closing, factors, traded, twins, screened, kept)
     shares = lax.all_to_all(total, PAIR, 0, 0, tiled=True)
     return jnp.sum(shares.astype(jnp.float32), axis=0)
 

time: 149 us -> 150 us (level)
  starting transfers between devices: 0.72 us -> 3.54 us
  waiting for transfers between devices: 26.5 us -> 23.7 us
    ppermute x2 -> x4, waiting for transfers between devices: 26.5 us -> 23.7 us  [the longest x2 23.7 us: shards(): traded.append(lax.ppermute(mine[:, b:b + 1], 'zh', swap))]
    ppermute x2 -> x4, starting transfers between devices: 0.72 us -> 3.54 us  [the longest x2 3.53 us: shards(): traded.append(lax.ppermute(mine[:, b:b + 1], 'zh', swap))]
  transfers between devices with their start and end apart: 3 -> 5, of which waited for: 1 -> 2; matrix products, arithmetic and copies ran while one was open for 0% -> 1% of each run, Pallas kernels for 14% -> 14%
where the time goes in v5:
time: 150 us
  blocking collectives  86.6 us (58%)
  Pallas kernels  31.5 us (21%)
  waiting for transfers between devices  23.7 us (16%)
  starting transfers between devices  3.54 us (2%)
  other arithmetic  2.71 us (2%)
    all_to_all x1, blocking collectives, shards(): mine = lax.all_to_all(picked, SAME_CORE, 0, 0, tiled=True)  47.8 us
    pallas_call x2, Pallas kernels, pair_sums(): pl.pallas_call(kernel, grid_spec=pltpu.PrefetchScalarGridSpec(num_scalar_...  28.7 us
    ppermute x2, waiting for transfers between devices, shards(): traded.append(lax.ppermute(mine[:, b:b + 1], 'zh', swap))  23.7 us
    all_to_all x1, blocking collectives, shards(): shares = lax.all_to_all(total, PAIR, 0, 0, tiled=True)  20.8 us
    all_to_all x1, blocking collectives, shards(): slices = lax.all_to_all(sent, PAIR, 0, 0, tiled=True)  18 us
    ppermute x2, starting transfers between devices, shards(): traded.append(lax.ppermute(mine[:, b:b + 1], 'zh', swap))  3.53 us
  transfers between devices with their start and end apart: 5, of which 2 were waited for; matrix products, arithmetic and copies ran while one was open for 1% of the time, Pallas kernels for 14%

profile of v5, /device:TPU:0, one launch (start us, length us, event | category | flops | bytes accessed | tf_op | source)
XLA Modules:
  0.0 149.6 jit_solution(18262690751644739158)
XLA Ops:
  0.0 0.7 convert_element_type.27
  0.7 0.1 copy.13
  0.8 0.1 convert_element_type.28
  0.9 1.0 pad_maximum_fusion
  1.9 18.0 %all_to_all.15.slices_ref = bf16[32,40,128]{2,1,0:T(8,128)(2,1)S(1)} all-to-all(bf16[32,40,128]{2,1,0:T(8,128)(2,1)S(1)} %pad_maximum_fusion), channel_id=1, replica_groups=mesh['zh'=2,'core'=2,'zl'=2,'y'=4,'x'=4] {'zl','y','x'}, dimensions={0} | all-to-all | bytes 655360 | tf_op jit(solution)/shard_map/all_to_all | solution.py:210
  20.0 2.8 %shard_map.46 = bf16[2,32,6,32,128]{4,3,2,1,0:T(8,128)(2,1)} custom-call(s32[32,8]{1,0:T(8,128)S(1)} %bitcast.17, bf16[32,40,128]{2,1,0:T(8,128)(2,1)S(1)} %all_to_all.15.slices_ref), custom_call_target="tpu_custom_call" | custom-call | tf_op jit(solution)/shard_map/pallas_call | solution.py:39
  22.8 0.0 copy-start
  22.8 0.0 copy-start.1
  22.8 47.8 %all_to_all.16 = bf16[64,6,32,128]{3,2,1,0:T(8,128)(2,1)S(1)} all-to-all(bf16[64,6,32,128]{3,2,1,0:T(8,128)(2,1)} %bitcast.18), channel_id=1, replica_groups=mesh['zh'=2,'core'=2,'zl'=2,'y'=4,'x'=4] {'zh','zl','y','x'}, dimensions={0} | all-to-all | bytes 6291456 | tf_op jit(solution)/shard_map/all_to_all | solution.py:221
  70.6 0.0 collective-permute-start.4
  70.6 1.1 fusion.2
  71.7 0.6 collective-permute-start
  72.3 2.9 %collective-permute-start.1 = (bf16[64,1,32,128]{3,2,1,0:T(8,128)(2,1)}, bf16[64,1,32,128]{3,2,1,0:T(8,128)(2,1)}, u32[]{:S(2)}, u32[]{:S(2)}) collective-permute-start(bf16[64,1,32,128]{3,2,1,0:T(8,128)(2,1)} %get-tuple-element.21), channel_id=1, source_target_pairs={{0,64},{64,0},{1,65},{65,1},{2,66},{66,2},{3,67},{67,3},{4,68},{68... | collective-permute-start | bytes 1572872 | tf_op jit(solution)/shard_map/ppermute | solution.py:231
  75.2 0.0 copy-done
  75.2 0.1 stack.21.where_ref
  75.3 0.1 pad_add_fusion.where_ref
  75.4 0.0 copy-done.1
  75.4 12.9 %collective-permute-done = bf16[64,1,32,128]{3,2,1,0:T(8,128)(2,1)} collective-permute-done((bf16[64,1,32,128]{3,2,1,0:T(8,128)(2,1)}, bf16[64,1,32,128]{3,2,1,0:T(8,128)(2,1)}, u32[]{:S(2)}, u32[]{:S(2)}) %collective-permute-start) | collective-permute-done | bytes 524320 | tf_op jit(solution)/shard_map/ppermute | solution.py:231
  88.3 0.0 collective-permute-start.2
  88.3 10.8 %collective-permute-done.1 = bf16[64,1,32,128]{3,2,1,0:T(8,128)(2,1)} collective-permute-done((bf16[64,1,32,128]{3,2,1,0:T(8,128)(2,1)}, bf16[64,1,32,128]{3,2,1,0:T(8,128)(2,1)}, u32[]{:S(2)}, u32[]{:S(2)}) %collective-permute-start.1) | collective-permute-done | bytes 524320 | tf_op jit(solution)/shard_map/ppermute | solution.py:231
  99.1 0.0 collective-permute-start.3
  99.1 0.1 exponential_multiply_fusion
  99.2 0.1 broadcast_multiply_fusion.fac
  99.2 0.0 collective-permute-done.4
  99.2 20.9 %shard_map.47 = (f32[2,512,512]{2,1,0:T(8,128)S(1)}, bf16[2,1024,1024]{2,1,0:T(8,128)(2,1)S(1)}) custom-call(s32[5]{0:T(128)S(1)} %stack.21.where_ref, f32[4,2,512]{2,1,0:T(2,128)S(1)} %broadcast_multiply_fusion.fac, bf16[2,32,6,32,128]{4,3,2,1,0:T(8,128)(2,1)S(1)} %bitcast.14, bf16[2,32,6,32,128]{4,3,2,1,0:T(8,128)(2,1)} %bitcast.12.refs_1_, ...), custom_call_target="tpu_custom_call" | custom-call | tf_op jit(solution)/shard_map/pallas_call | solution.py:174
  120.2 0.0 collective-permute-done.2
  120.2 0.0 collective-permute-done.3
  120.2 7.8 %shard_map.48 = bf16[32,2,16,512]{3,2,1,0:T(8,128)(2,1)S(1)} custom-call(s32[2]{0:T(128)S(1)} %pad_add_fusion.where_ref, f32[4,2,512]{2,1,0:T(2,128)S(1)} %broadcast_multiply_fusion.fac, bf16[2,32,1,32,128]{4,3,2,1,0:T(8,128)(2,1)} %bitcast.6.refs_0_, bf16[2,32,1,32,128]{4,3,2,1,0:T(8,128)(2,1)} %bitcast.7.refs_1_, ...), custom_call_target="tpu_custom_call" | custom-call | tf_op jit(solution)/shard_map/pallas_call | solution.py:174
  128.0 20.8 %all_to_all.17 = bf16[32,2,16,512]{3,2,1,0:T(8,128)(2,1)S(1)} all-to-all(bf16[32,2,16,512]{3,2,1,0:T(8,128)(2,1)S(1)} %shard_map.48), channel_id=1, replica_groups=mesh['zh'=2,'core'=2,'zl'=2,'y'=4,'x'=4] {'zl','y','x'}, dimensions={0} | all-to-all | bytes 2097152 | tf_op jit(solution)/shard_map/all_to_all | solution.py:241
  148.8 0.8 convert_reduce_fusion
  (7 shorter events, 0.1 us)
Async XLA Ops:
  22.8 52.4 %copy-start = (f32[512]{0:T(512)S(1)}, f32[512]{0:T(512)}, u32[]{:S(2)}) copy-start(f32[512]{0:T(512)} %param.7) | copy-start | bytes 6148
  22.8 52.6 %copy-start.1 = (s32[4,2]{0,1:T(2,128)S(1)}, s32[4,2]{0,1:T(2,128)}, u32[]{:S(2)}) copy-start(s32[4,2]{0,1:T(2,128)} %param.9) | copy-start | bytes 100
  70.6 28.6 %collective-permute-start.4 = (bf16[64,6,32,128]{3,2,1,0:T(8,128)(2,1)S(1)}, bf16[64,6,32,128]{3,2,1,0:T(8,128)(2,1)}, u32[]{:S(2)}, u32[]{:S(2)}) collective-permute-start(bf16[64,6,32,128]{3,2,1,0:T(8,128)(2,1)S(1)} %all_to_all.16), channel_id=1, source_target_pairs={{0,32},{32,0},{1,33},{33,1},{2,34},{34,2},{3,35},{35,3},{4,36},{36... | collective-permute-start | bytes 9437192 | tf_op jit(solution)/shard_map/ppermute | solution.py:228
  71.7 16.6 %collective-permute-start = (bf16[64,1,32,128]{3,2,1,0:T(8,128)(2,1)}, bf16[64,1,32,128]{3,2,1,0:T(8,128)(2,1)}, u32[]{:S(2)}, u32[]{:S(2)}) collective-permute-start(bf16[64,1,32,128]{3,2,1,0:T(8,128)(2,1)} %get-tuple-element.22), channel_id=1, source_target_pairs={{0,64},{64,0},{1,65},{65,1},{2,66},{66,2},{3,67},{67,3},{4,68},{68... | collective-permute-start | bytes 1572872 | tf_op jit(solution)/shard_map/ppermute | solution.py:231
  72.3 26.8 %collective-permute-start.1 = (bf16[64,1,32,128]{3,2,1,0:T(8,128)(2,1)}, bf16[64,1,32,128]{3,2,1,0:T(8,128)(2,1)}, u32[]{:S(2)}, u32[]{:S(2)}) collective-permute-start(bf16[64,1,32,128]{3,2,1,0:T(8,128)(2,1)} %get-tuple-element.21), channel_id=1, source_target_pairs={{0,64},{64,0},{1,65},{65,1},{2,66},{66,2},{3,67},{67,3},{4,68},{68... | collective-permute-start | bytes 1572872 | tf_op jit(solution)/shard_map/ppermute | solution.py:231
  88.3 31.9 %collective-permute-start.2 = (bf16[64,1,32,128]{3,2,1,0:T(8,128)(2,1)}, bf16[64,1,32,128]{3,2,1,0:T(8,128)(2,1)S(1)}, u32[]{:S(2)}, u32[]{:S(2)}) collective-permute-start(bf16[64,1,32,128]{3,2,1,0:T(8,128)(2,1)} %collective-permute-done), channel_id=1, source_target_pairs={{0,32},{32,0},{1,33},{33,1},{2,34},{34,2},{3,35},{35,3},{4,36},{36... | collective-permute-start | bytes 1572872 | tf_op jit(solution)/shard_map/ppermute | solution.py:237
  99.1 21.1 %collective-permute-start.3 = (bf16[64,1,32,128]{3,2,1,0:T(8,128)(2,1)}, bf16[64,1,32,128]{3,2,1,0:T(8,128)(2,1)S(1)}, u32[]{:S(2)}, u32[]{:S(2)}) collective-permute-start(bf16[64,1,32,128]{3,2,1,0:T(8,128)(2,1)} %collective-permute-done.1), channel_id=1, source_target_pairs={{0,32},{32,0},{1,33},{33,1},{2,34},{34,2},{3,35},{35,3},{4,36},{36... | collective-permute-start | bytes 1572872 | tf_op jit(solution)/shard_map/ppermute | solution.py:237

commit v6 on v5

--- a/solution.py
+++ b/solution.py
@@ -27,7 +27,7 @@
             for d in range(per_step):
                 for half in range(2):
                     for k in range(count):
-                        block = wants_ref[i * per_step + d, 2 * FIRST[half][k // 2] + k % 2]
+                        block = wants_ref[i * per_step + d, k % 2, FIRST[half][k // 2]]
                         piece = slices_ref.at[block, pl.ds(0, rows), :]
                         at = out_ref.at[half, i * per_step + d, k]
                         pltpu.make_async_copy(piece, at, sent).start()
@@ -199,7 +199,7 @@
     norb = level_gap.shape[0]
 
     asked = jnp.zeros((INDEX_ROWS, cols), jnp.bfloat16)
-    asked = asked.at[0, : 2 * pair_local].set(pair_blocks.reshape(-1).astype(jnp.bfloat16))
+    asked = asked.at[:2, :pair_local].set(pair_blocks.T.astype(jnp.bfloat16))
     sent = jnp.concatenate(
         [
             orbitals.reshape(owners, rows, cols),
@@ -208,7 +208,7 @@
         axis=1,
     )
     slices = lax.all_to_all(sent, PAIR, 0, 0, tiled=True)
-    wants = slices[:, rows, : 2 * pair_local].astype(jnp.int32)
+    wants = slices[:, rows : rows + 2, :pair_local].astype(jnp.int32)
 
     half = lax.axis_index("zh")
     core = lax.axis_index("core")

time: 150 us -> 150 us (level)
  no operation moved by 1% of the time
where the time goes in v6:
time: 150 us
  blocking collectives  86.6 us (58%)
  Pallas kernels  31.8 us (21%)
  waiting for transfers between devices  23.7 us (16%)
  starting transfers between devices  3.54 us (2%)
  other arithmetic  2.71 us (2%)
    all_to_all x1, blocking collectives, shards(): mine = lax.all_to_all(picked, SAME_CORE, 0, 0, tiled=True)  47.8 us
    pallas_call x2, Pallas kernels, pair_sums(): pl.pallas_call(kernel, grid_spec=pltpu.PrefetchScalarGridSpec(num_scalar_...  28.7 us
    ppermute x2, waiting for transfers between devices, shards(): traded.append(lax.ppermute(mine[:, b:b + 1], 'zh', swap))  23.7 us
    all_to_all x1, blocking collectives, shards(): shares = lax.all_to_all(total, PAIR, 0, 0, tiled=True)  20.8 us
    all_to_all x1, blocking collectives, shards(): slices = lax.all_to_all(sent, PAIR, 0, 0, tiled=True)  18 us
    ppermute x2, starting transfers between devices, shards(): traded.append(lax.ppermute(mine[:, b:b + 1], 'zh', swap))  3.53 us
    pallas_call x1, Pallas kernels, picked_for(): pl.pallas_call(kernel, grid_spec=pltpu.PrefetchScalarGridSpec(num_scalar_...  3.1 us
  transfers between devices with their start and end apart: 5, of which 2 were waited for; matrix products, arithmetic and copies ran while one was open for 1% of the time, Pallas kernels for 14%

profile of v6, /device:TPU:0, one launch (start us, length us, event | category | flops | bytes accessed | tf_op | source)
XLA Modules:
  0.0 149.6 jit_solution(566956879121371884)
XLA Ops:
  0.0 0.7 convert_bitcast_fusion
  0.7 1.0 pad_maximum_fusion
  1.7 18.0 %all_to_all.15.slices_ref = bf16[32,40,128]{2,1,0:T(8,128)(2,1)S(1)} all-to-all(bf16[32,40,128]{2,1,0:T(8,128)(2,1)S(1)} %pad_maximum_fusion), channel_id=1, replica_groups=mesh['zh'=2,'core'=2,'zl'=2,'y'=4,'x'=4] {'zl','y','x'}, dimensions={0} | all-to-all | bytes 655360 | tf_op jit(solution)/shard_map/all_to_all | solution.py:210
  19.8 3.1 %shard_map.46 = bf16[2,32,6,32,128]{4,3,2,1,0:T(8,128)(2,1)} custom-call(s32[32,2,4]{2,1,0:T(2,128)S(1)} %slice_convert_fusion.wants_ref, bf16[32,40,128]{2,1,0:T(8,128)(2,1)S(1)} %all_to_all.15.slices_ref), custom_call_target="tpu_custom_call" | custom-call | tf_op jit(solution)/shard_map/pallas_call | solution.py:39
  22.9 0.0 copy-start
  22.9 0.0 copy-start.1
  22.9 47.8 %all_to_all.16 = bf16[64,6,32,128]{3,2,1,0:T(8,128)(2,1)S(1)} all-to-all(bf16[64,6,32,128]{3,2,1,0:T(8,128)(2,1)} %bitcast.18), channel_id=1, replica_groups=mesh['zh'=2,'core'=2,'zl'=2,'y'=4,'x'=4] {'zh','zl','y','x'}, dimensions={0} | all-to-all | bytes 6291456 | tf_op jit(solution)/shard_map/all_to_all | solution.py:221
  70.7 0.0 collective-permute-start.4
  70.7 1.1 fusion.2
  71.8 0.6 collective-permute-start
  72.4 2.9 %collective-permute-start.1 = (bf16[64,1,32,128]{3,2,1,0:T(8,128)(2,1)}, bf16[64,1,32,128]{3,2,1,0:T(8,128)(2,1)}, u32[]{:S(2)}, u32[]{:S(2)}) collective-permute-start(bf16[64,1,32,128]{3,2,1,0:T(8,128)(2,1)} %get-tuple-element.21), channel_id=1, source_target_pairs={{0,64},{64,0},{1,65},{65,1},{2,66},{66,2},{3,67},{67,3},{4,68},{68... | collective-permute-start | bytes 1572872 | tf_op jit(solution)/shard_map/ppermute | solution.py:231
  75.3 0.0 copy-done
  75.3 0.1 stack.21.where_ref
  75.4 0.1 pad_add_fusion.where_ref
  75.5 0.0 copy-done.1
  75.5 12.9 %collective-permute-done = bf16[64,1,32,128]{3,2,1,0:T(8,128)(2,1)} collective-permute-done((bf16[64,1,32,128]{3,2,1,0:T(8,128)(2,1)}, bf16[64,1,32,128]{3,2,1,0:T(8,128)(2,1)}, u32[]{:S(2)}, u32[]{:S(2)}) %collective-permute-start) | collective-permute-done | bytes 524320 | tf_op jit(solution)/shard_map/ppermute | solution.py:231
  88.4 0.0 collective-permute-start.2
  88.4 10.8 %collective-permute-done.1 = bf16[64,1,32,128]{3,2,1,0:T(8,128)(2,1)} collective-permute-done((bf16[64,1,32,128]{3,2,1,0:T(8,128)(2,1)}, bf16[64,1,32,128]{3,2,1,0:T(8,128)(2,1)}, u32[]{:S(2)}, u32[]{:S(2)}) %collective-permute-start.1) | collective-permute-done | bytes 524320 | tf_op jit(solution)/shard_map/ppermute | solution.py:231
  99.1 0.0 collective-permute-start.3
  99.2 0.1 exponential_multiply_fusion
  99.2 0.1 broadcast_multiply_fusion.fac
  99.3 0.0 collective-permute-done.4
  99.3 20.9 %shard_map.47 = (f32[2,512,512]{2,1,0:T(8,128)S(1)}, bf16[2,1024,1024]{2,1,0:T(8,128)(2,1)S(1)}) custom-call(s32[5]{0:T(128)S(1)} %stack.21.where_ref, f32[4,2,512]{2,1,0:T(2,128)S(1)} %broadcast_multiply_fusion.fac, bf16[2,32,6,32,128]{4,3,2,1,0:T(8,128)(2,1)S(1)} %bitcast.15, bf16[2,32,6,32,128]{4,3,2,1,0:T(8,128)(2,1)} %bitcast.12.refs_1_, ...), custom_call_target="tpu_custom_call" | custom-call | tf_op jit(solution)/shard_map/pallas_call | solution.py:174
  120.2 0.0 collective-permute-done.2
  120.2 0.0 collective-permute-done.3
  120.3 7.8 %shard_map.48 = bf16[32,2,16,512]{3,2,1,0:T(8,128)(2,1)S(1)} custom-call(s32[2]{0:T(128)S(1)} %pad_add_fusion.where_ref, f32[4,2,512]{2,1,0:T(2,128)S(1)} %broadcast_multiply_fusion.fac, bf16[2,32,1,32,128]{4,3,2,1,0:T(8,128)(2,1)} %bitcast.6.refs_0_, bf16[2,32,1,32,128]{4,3,2,1,0:T(8,128)(2,1)} %bitcast.7.refs_1_, ...), custom_call_target="tpu_custom_call" | custom-call | tf_op jit(solution)/shard_map/pallas_call | solution.py:174
  128.0 20.8 %all_to_all.17 = bf16[32,2,16,512]{3,2,1,0:T(8,128)(2,1)S(1)} all-to-all(bf16[32,2,16,512]{3,2,1,0:T(8,128)(2,1)S(1)} %shard_map.48), channel_id=1, replica_groups=mesh['zh'=2,'core'=2,'zl'=2,'y'=4,'x'=4] {'zl','y','x'}, dimensions={0} | all-to-all | bytes 2097152 | tf_op jit(solution)/shard_map/all_to_all | solution.py:241
  148.8 0.8 convert_reduce_fusion
  (7 shorter events, 0.1 us)
Async XLA Ops:
  22.9 52.4 %copy-start = (f32[512]{0:T(512)S(1)}, f32[512]{0:T(512)}, u32[]{:S(2)}) copy-start(f32[512]{0:T(512)} %param.7) | copy-start | bytes 6148
  22.9 52.6 %copy-start.1 = (s32[4,2]{0,1:T(2,128)S(1)}, s32[4,2]{0,1:T(2,128)}, u32[]{:S(2)}) copy-start(s32[4,2]{0,1:T(2,128)} %param.9) | copy-start | bytes 100
  70.7 28.6 %collective-permute-start.4 = (bf16[64,6,32,128]{3,2,1,0:T(8,128)(2,1)S(1)}, bf16[64,6,32,128]{3,2,1,0:T(8,128)(2,1)}, u32[]{:S(2)}, u32[]{:S(2)}) collective-permute-start(bf16[64,6,32,128]{3,2,1,0:T(8,128)(2,1)S(1)} %all_to_all.16), channel_id=1, source_target_pairs={{0,32},{32,0},{1,33},{33,1},{2,34},{34,2},{3,35},{35,3},{4,36},{36... | collective-permute-start | bytes 9437192 | tf_op jit(solution)/shard_map/ppermute | solution.py:228
  71.8 16.6 %collective-permute-start = (bf16[64,1,32,128]{3,2,1,0:T(8,128)(2,1)}, bf16[64,1,32,128]{3,2,1,0:T(8,128)(2,1)}, u32[]{:S(2)}, u32[]{:S(2)}) collective-permute-start(bf16[64,1,32,128]{3,2,1,0:T(8,128)(2,1)} %get-tuple-element.22), channel_id=1, source_target_pairs={{0,64},{64,0},{1,65},{65,1},{2,66},{66,2},{3,67},{67,3},{4,68},{68... | collective-permute-start | bytes 1572872 | tf_op jit(solution)/shard_map/ppermute | solution.py:231
  72.4 26.8 %collective-permute-start.1 = (bf16[64,1,32,128]{3,2,1,0:T(8,128)(2,1)}, bf16[64,1,32,128]{3,2,1,0:T(8,128)(2,1)}, u32[]{:S(2)}, u32[]{:S(2)}) collective-permute-start(bf16[64,1,32,128]{3,2,1,0:T(8,128)(2,1)} %get-tuple-element.21), channel_id=1, source_target_pairs={{0,64},{64,0},{1,65},{65,1},{2,66},{66,2},{3,67},{67,3},{4,68},{68... | collective-permute-start | bytes 1572872 | tf_op jit(solution)/shard_map/ppermute | solution.py:231
  88.4 31.9 %collective-permute-start.2 = (bf16[64,1,32,128]{3,2,1,0:T(8,128)(2,1)}, bf16[64,1,32,128]{3,2,1,0:T(8,128)(2,1)S(1)}, u32[]{:S(2)}, u32[]{:S(2)}) collective-permute-start(bf16[64,1,32,128]{3,2,1,0:T(8,128)(2,1)} %collective-permute-done), channel_id=1, source_target_pairs={{0,32},{32,0},{1,33},{33,1},{2,34},{34,2},{3,35},{35,3},{4,36},{36... | collective-permute-start | bytes 1572872 | tf_op jit(solution)/shard_map/ppermute | solution.py:237
  99.1 21.1 %collective-permute-start.3 = (bf16[64,1,32,128]{3,2,1,0:T(8,128)(2,1)}, bf16[64,1,32,128]{3,2,1,0:T(8,128)(2,1)S(1)}, u32[]{:S(2)}, u32[]{:S(2)}) collective-permute-start(bf16[64,1,32,128]{3,2,1,0:T(8,128)(2,1)} %collective-permute-done.1), channel_id=1, source_target_pairs={{0,32},{32,0},{1,33},{33,1},{2,34},{34,2},{3,35},{35,3},{4,36},{36... | collective-permute-start | bytes 1572872 | tf_op jit(solution)/shard_map/ppermute | solution.py:237
